TPU v7x, 256 devices: a whole 4x4x8 slice. The times are simulated.
256 devices in a mesh: tok: 32 (over x, y, core), feat: 8 (over z).
Axes of the slice: x: 4, y: 4, z: 8, core: 2. Of those that a mesh axis runs over, the one named last changes fastest.
Arguments:
- inputs: bfloat16 [16384, 2048], P(('tok', 'feat'))
- norm_gain: float32 [2048], replicated, may hold values from 0.1 to 1.9
- w_in: bfloat16 [512, 8192], P('tok', 'feat'), may hold values from -0.25 to 0.25
- w_out: bfloat16 [512, 8192], P('tok', 'feat'), may hold values from -0.125 to 0.125
- block_index: int32 [64, 4], P('feat'), may hold values from 0 to 15, all different within a row
- segment_ids: int32 [16384], P(('tok', 'feat')), may hold values from 0 to 1023, never falling along the last dimension, each value on 1 to 24 neighbouring positions
- teacher_scores: float32 [1024], replicated, may hold values from -6 to 6
- upstream: bfloat16 [16384, 2048], P(('tok', 'feat')), may hold values from -6 to 6
- readout: float32 [2048], replicated, may hold values from -0.125 to 0.125
Outputs:
- layer_out: bfloat16 [16384, 2048], P(('tok', 'feat'))
- input_grad: bfloat16 [16384, 2048], P(('tok', 'feat'))
- grad_in: float32 [512, 8192], P('tok', 'feat')
- grad_out: float32 [512, 8192], P('tok', 'feat')
Inputs may be any that keep to these rules, and one draw needn't show every extreme that they name: `block_index`: each row names 4 different feature blocks; every feature block is named by some row. `segment_ids`: never falls along the tokens; every segment 0 to 1023 holds 1 to 24 tokens.
All inputs are finite; a program needn't handle non-finite values.
Results may differ from a plain program's by a relative error of at most 0.015.
Values may be sent and summed in bfloat16 or wider, within the bound.
A program may use at most 128 MiB of HBM per device.

v0:
```python
import math

import jax
import jax.numpy as jnp
from jax import lax
from jax.sharding import PartitionSpec as P

BLK = 128


EPS = 1e-06
LOSS_WEIGHT = 8.0


def gelu_tanh(values):
    return jax.nn.gelu(values, approximate=True)


def gelu_back(values, cotangent):
    return jax.vjp(gelu_tanh, values)[1](cotangent)[0]


def on_device(
    inputs, norm_gain, w_in, w_out, block_index, segment_ids, teacher_scores, upstream, readout
):
    local_tokens, model_width = inputs.shape
    blocks_here = w_in.shape[1] // BLK
    feature_blocks = model_width // BLK
    per_hidden = block_index.shape[1]
    total_tokens = local_tokens * lax.axis_size("tok") * lax.axis_size("feat")
    grad_scale = 1.0 / math.sqrt(total_tokens)
    inputs_wide = inputs.astype(jnp.float32)
    mean_square = jnp.mean(inputs_wide * inputs_wide, axis=1, keepdims=True)
    inv_rms = lax.rsqrt(mean_square + EPS)
    normed = (inputs_wide * inv_rms * norm_gain[None, :]).astype(jnp.bfloat16)
    w_in_all, w_out_all = (
        lax.all_gather(w_in, "tok", axis=0, tiled=True),
        lax.all_gather(w_out, "tok", axis=0, tiled=True),
    )
    picked_width = w_in_all.shape[0]
    w_in_blocks = w_in_all.reshape(picked_width, blocks_here, BLK)
    w_out_blocks = w_out_all.reshape(picked_width, blocks_here, BLK)
    normed_rows = lax.all_gather(normed, "feat", axis=0, tiled=True)
    group_rows = normed_rows.shape[0]
    one_hot = block_index[:, :, None] == jnp.arange(feature_blocks, dtype=jnp.int32)[None, None, :]
    sel_half = one_hot.astype(jnp.bfloat16)
    sel_wide = one_hot.astype(jnp.float32)

    def select(rows):
        blocks = rows.reshape(group_rows, feature_blocks, BLK)
        picked = jnp.einsum("rdc,jkd->rjkc", blocks, sel_half, preferred_element_type=jnp.float32)
        return picked.astype(jnp.bfloat16).reshape(group_rows, blocks_here, picked_width)

    def spread(terms):
        grouped = terms.reshape(group_rows, blocks_here, per_hidden, BLK)
        placed = jnp.einsum("rjkc,jkd->rdc", grouped, sel_wide, precision=lax.Precision.HIGHEST)
        return placed.reshape(group_rows, model_width)

    chosen = select(normed_rows)
    pre_act = jnp.einsum("rjm,mjc->rjc", chosen, w_in_blocks, preferred_element_type=jnp.float32)
    activated = gelu_tanh(pre_act).astype(jnp.bfloat16)
    out_terms_fwd = jnp.einsum(
        "rjc,mjc->rjm", activated, w_out_blocks, preferred_element_type=jnp.float32
    )
    branch = lax.psum_scatter(
        spread(out_terms_fwd).astype(jnp.bfloat16), "feat", scatter_dimension=0, tiled=True
    ).astype(jnp.float32)
    layer_out = (inputs_wide + branch).astype(jnp.bfloat16)
    token_score = jnp.dot(layer_out.astype(jnp.float32), readout, precision=lax.Precision.HIGHEST)
    segment_count = teacher_scores.shape[0]
    member = (segment_ids[:, None] == jnp.arange(segment_count, dtype=jnp.int32)[None, :]).astype(
        jnp.float32
    )
    score_sums = jnp.dot(token_score, member, precision=lax.Precision.HIGHEST)
    token_counts = jnp.sum(member, axis=0)
    score_sums, token_counts = lax.psum((score_sums, token_counts), ("tok", "feat"))
    misfit = score_sums / token_counts - teacher_scores
    token_coeff = 2.0 * LOSS_WEIGHT * jnp.sum(member * misfit[None, :], axis=1)
    cotangent_local = (
        upstream.astype(jnp.float32) + token_coeff[:, None] * readout[None, :]
    ).astype(jnp.bfloat16)
    cotangent_rows = lax.all_gather(cotangent_local, "feat", axis=0, tiled=True)
    chosen_grad = select(cotangent_rows)
    upper_grad = jnp.einsum(
        "rjm,mjc->rjc", chosen_grad, w_out_blocks, preferred_element_type=jnp.float32
    )
    pre_grad = gelu_back(pre_act, upper_grad).astype(jnp.bfloat16)

    def arrange(terms):
        return terms.reshape(picked_width, blocks_here * BLK) * grad_scale

    back_terms = jnp.einsum(
        "rjc,mjc->rjm", pre_grad, w_in_blocks, preferred_element_type=jnp.float32
    )
    out_terms = jnp.einsum(
        "rjm,rjc->mjc", chosen_grad, activated, preferred_element_type=jnp.float32
    )
    in_terms = jnp.einsum("rjm,rjc->mjc", chosen, pre_grad, preferred_element_type=jnp.float32)
    grad_out, grad_in = (
        lax.psum_scatter(
            arrange(out_terms).astype(jnp.bfloat16), "tok", scatter_dimension=0, tiled=True
        ).astype(jnp.float32),
        lax.psum_scatter(
            arrange(in_terms).astype(jnp.bfloat16), "tok", scatter_dimension=0, tiled=True
        ).astype(jnp.float32),
    )
    back_sum = lax.psum_scatter(
        spread(back_terms).astype(jnp.bfloat16), "feat", scatter_dimension=0, tiled=True
    ).astype(jnp.float32)
    scaled = back_sum * norm_gain[None, :]
    inner_mean = jnp.mean(scaled * inputs_wide, axis=1, keepdims=True)
    norm_back = inv_rms * scaled - inputs_wide * (inv_rms * inv_rms * inv_rms) * inner_mean
    input_grad = (cotangent_local.astype(jnp.float32) + norm_back).astype(jnp.bfloat16)
    return (layer_out, input_grad, grad_in, grad_out)


def solution(mesh):
    return jax.shard_map(
        on_device,
        mesh=mesh,
        in_specs=(
            P(("tok", "feat"), None),
            P(),
            P("tok", "feat"),
            P("tok", "feat"),
            P("feat", None),
            P(("tok", "feat")),
            P(),
            P(("tok", "feat"), None),
            P(),
        ),
        out_specs=(
            P(("tok", "feat"), None),
            P(("tok", "feat"), None),
            P("tok", "feat"),
            P("tok", "feat"),
        ),
        check_vma=False,
    )
```

profile of v0, /device:TPU:1, one launch (start us, length us, event | category | flops | bytes accessed | tf_op | source)
XLA Modules:
  0.0 577.8 jit_solution(5638336384249948303)
XLA Ops:
  7.2 0.0 all-gather.7.cloned.1.call-start
  7.2 0.7 all-gather.7.cloned.1.call-update
  7.9 0.0 all-gather.9.cloned.1.call-start
  7.9 0.7 all-gather.9.cloned.1.call-update
  8.6 0.0 all-gather.5.cloned.1.call-start
  8.7 1.1 fusion.25
  9.8 1.8 fusion.27
  11.6 0.0 all-gather.5.cloned.1.call-update
  11.6 0.0 reduce-scatter.5.cloned.1.call-start
  11.7 50.6 %all-gather.7.cloned.1.call-done = bf16[512,1024]{1,0:T(8,128)(2,1)} async-done(((bf16[16,1024]{1,0:T(8,128)(2,1)}), bf16[512,1024]{1,0:T(8,128)(2,1)}) %all-gather.7.cloned.1.call-update) | async-done | bytes 1048592 | tf_op jit(solution)/shard_map/all_gather | solution.py:37
  62.3 1.5 copy.56
  63.8 48.1 %all-gather.9.cloned.1.call-done = bf16[512,1024]{1,0:T(8,128)(2,1)} async-done(((bf16[16,1024]{1,0:T(8,128)(2,1)}), bf16[512,1024]{1,0:T(8,128)(2,1)}) %all-gather.9.cloned.1.call-update) | async-done | bytes 1048592 | tf_op jit(solution)/shard_map/all_gather | solution.py:38
  111.8 1.5 copy.59
  113.3 36.6 %all-gather.5.cloned.1.call-done = bf16[512,2048]{1,0:T(8,128)(2,1)} async-done(((bf16[64,2048]{1,0:T(8,128)(2,1)}), bf16[512,2048]{1,0:T(8,128)(2,1)}) %all-gather.5.cloned.1.call-update) | async-done | bytes 2097168 | tf_op jit(solution)/shard_map/all_gather | solution.py:43
  150.0 2.2 copy.82
  152.2 1.3 convert_bitcast_fusion.1
  153.5 0.7 copy.105
  154.2 1.4 fusion.6
  155.6 0.6 copy-done.1
  156.2 4.6 fusion.47
  160.7 10.4 %copy.61 = f32[512,8,4,128]{3,1,2,0:T(8,128)} copy(f32[512,8,4,128]{0,3,2,1:T(8,128)} %bitcast.104) | data formatting | bytes 16777216 | tf_op jit(solution)/shard_map/reshape | solution.py:55
  171.2 5.6 bitcast_convert_fusion.1
  176.8 1.9 copy.107
  178.7 0.0 reduce-scatter.5.cloned.1.call-update
  178.7 0.0 all-gather.11.cloned.1.call-start
  178.7 0.6 copy-done.16
  179.3 0.1 convert_reduce_fusion
  179.4 40.6 %reduce-scatter.5.cloned.1.call-done = bf16[64,2048]{1,0:T(8,128)(2,1)} async-done(((bf16[512,2048]{1,0:T(8,128)(2,1)}), bf16[64,2048]{1,0:T(8,128)(2,1)}) %reduce-scatter.5.cloned.1.call-update) | async-done | bytes 262160 | tf_op jit(solution)/shard_map/reduce_scatter | solution.py:65
  220.0 1.0 fusion.28
  221.1 0.0 copy-start.11
  221.1 0.7 copy-done.11
  221.8 0.3 convolution_bitcast_fusion
  222.1 0.3 fusion.34
  222.3 79.0 %all-reduce = (f32[1024]{0:T(1024)S(1)}, f32[1024]{0:T(1024)S(1)}) all-reduce(f32[1024]{0:T(1024)S(1)} %bitcast.124, f32[1024]{0:T(1024)S(1)} %convert_reduce_fusion), channel_id=1, replica_groups=mesh['tok'=32,'feat'=8] {'tok','feat'}, use_global_device_ids=true, to_apply=%region_2.0 | all-reduce | flops 2048 | bytes 16384 | tf_op jit(solution)/shard_map/psum | solution.py:76
  301.4 0.2 select_reduce_fusion
  301.6 0.8 add_convert_fusion
  302.4 0.0 all-gather.11.cloned.1.call-update
  302.5 0.2 reduce-scatter.9.cloned.1.call-start
  302.7 33.0 %all-gather.11.cloned.1.call-done = bf16[512,2048]{1,0:T(8,128)(2,1)} async-done(((bf16[64,2048]{1,0:T(8,128)(2,1)}), bf16[512,2048]{1,0:T(8,128)(2,1)}) %all-gather.11.cloned.1.call-update) | async-done | bytes 2097168 | tf_op jit(solution)/shard_map/all_gather | solution.py:82
  335.7 2.2 copy.84
  337.9 1.3 convert_bitcast_fusion
  339.2 0.7 copy.104
  340.0 0.8 copy-done.5
  340.8 3.7 fusion.14
  344.5 3.6 multiply_convert_fusion.1
  348.1 2.4 copy.69
  350.6 0.0 reduce-scatter.9.cloned.1.call-update
  350.6 0.0 reduce-scatter.11.cloned.1.call-start
  350.6 6.2 %multiply_convert_fusion = bf16[8,128,512]{2,1,0:T(8,128)(2,1)} fusion(bf16[512,8,512]{2,1,0:T(8,128)(2,1)} %bitcast.116, f32[8,512,128]{2,1,0:T(8,128)S(1)} %copy-done.6), kind=kOutput, calls=%fused_computation.32 | convolution fusion | flops 542638080 | bytes 7340032 | tf_op jit(solution)/shard_map/rjm,rjc->mjc/dot_general | solution.py:95
  356.8 2.4 copy.72
  359.2 0.0 reduce-scatter.11.cloned.1.call-update
  359.2 0.3 reduce-scatter.7.cloned.1.call-start
  359.5 4.5 fusion.49
  364.0 10.5 %copy.66 = f32[512,8,4,128]{3,1,2,0:T(8,128)} copy(f32[512,8,4,128]{0,3,2,1:T(8,128)} %bitcast.103) | data formatting | bytes 16777216 | tf_op jit(solution)/shard_map/reshape | solution.py:55
  374.5 5.6 bitcast_convert_fusion
  380.1 1.9 copy.106
  382.0 0.0 reduce-scatter.7.cloned.1.call-update
  382.0 55.1 %reduce-scatter.9.cloned.1.call-done = bf16[16,1024]{1,0:T(8,128)(2,1)} async-done(((bf16[512,1024]{1,0:T(8,128)(2,1)}), bf16[16,1024]{1,0:T(8,128)(2,1)}) %reduce-scatter.9.cloned.1.call-update) | async-done | bytes 32784 | tf_op jit(solution)/shard_map/reduce_scatter | solution.py:103
  437.1 1.4 convert_element_type.118
  438.5 87.3 %reduce-scatter.11.cloned.1.call-done = bf16[16,1024]{1,0:T(8,128)(2,1)} async-done(((bf16[512,1024]{1,0:T(8,128)(2,1)}), bf16[16,1024]{1,0:T(8,128)(2,1)}) %reduce-scatter.11.cloned.1.call-update) | async-done | bytes 32784 | tf_op jit(solution)/shard_map/reduce_scatter | solution.py:100
  525.8 1.4 convert_element_type.122
  527.2 40.7 %reduce-scatter.7.cloned.1.call-done = bf16[64,2048]{1,0:T(8,128)(2,1)} async-done(((bf16[512,2048]{1,0:T(8,128)(2,1)}), bf16[64,2048]{1,0:T(8,128)(2,1)}) %reduce-scatter.7.cloned.1.call-update) | async-done | bytes 262160 | tf_op jit(solution)/shard_map/reduce_scatter | solution.py:107
  567.9 1.1 fusion.33
  569.0 2.0 fusion.32
  (33 shorter events, 0.1 us)
Async XLA Ops:
  7.2 55.1 %all-gather.7.cloned.1.call-start = ((), (), s32[]{:S(2)}) async-start(), calls=%async_computation.5 | async-start | bytes 1081344 | tf_op jit(solution)/shard_map/all_gather | solution.py:37
  7.9 103.9 %all-gather.9.cloned.1.call-start = ((), (), s32[]{:S(2)}) async-start(), calls=%async_computation.6 | async-start | bytes 1081344 | tf_op jit(solution)/shard_map/all_gather | solution.py:38
  8.6 141.3 %all-gather.5.cloned.1.call-start = ((), (), s32[]{:S(2)}) async-start(), calls=%async_computation.4 | async-start | bytes 2359296 | tf_op jit(solution)/shard_map/all_gather | solution.py:43
  11.6 208.4 %reduce-scatter.5.cloned.1.call-start = ((), (), s32[]{:S(2)}) async-start(), calls=%async_computation.7 | async-start | bytes 2359296 | tf_op jit(solution)/shard_map/reduce_scatter | solution.py:65
  150.0 2.2 copy-start.12
  154.2 2.0 copy-start.1
  156.2 4.6 copy-start.4
  178.6 0.7 copy-start.16
  178.6 41.4 %copy-start = (bf16[64,2048]{1,0:T(8,128)(2,1)S(1)}, bf16[64,2048]{1,0:T(8,128)(2,1)}, u32[]{:S(2)}) copy-start(bf16[64,2048]{1,0:T(8,128)(2,1)} %param.9) | copy-start | bytes 786436
  178.6 43.1 %copy-start.14 = (f32[2048]{0:T(1024)S(1)}, f32[2048]{0:T(1024)}, u32[]{:S(2)}) copy-start(f32[2048]{0:T(1024)} %param.17) | copy-start | bytes 24580
  178.6 122.8 %copy-start.15 = (f32[1024]{0:T(1024)S(1)}, f32[1024]{0:T(1024)}, u32[]{:S(2)}) copy-start(f32[1024]{0:T(1024)} %param.15) | copy-start | bytes 12292
  178.6 123.0 %copy-start.9 = (bf16[64,2048]{1,0:T(8,128)(2,1)S(1)}, bf16[64,2048]{1,0:T(8,128)(2,1)}, u32[]{:S(2)}) copy-start(bf16[64,2048]{1,0:T(8,128)(2,1)} %param.16) | copy-start | bytes 786436
  178.7 157.0 %all-gather.11.cloned.1.call-start = ((), (), s32[]{:S(2)}) async-start(), calls=%async_computation.8 | async-start | bytes 2359296 | tf_op jit(solution)/shard_map/all_gather | solution.py:82
  221.1 0.7 copy-start.11
  302.5 134.6 %reduce-scatter.9.cloned.1.call-start = ((), (), s32[]{:S(2)}) async-start(), calls=%async_computation.10 | async-start | bytes 1081344 | tf_op jit(solution)/shard_map/reduce_scatter | solution.py:103
  339.2 1.6 copy-start.5
  339.9 4.5 copy-start.3
  340.8 3.7 copy-start.2
  344.5 3.6 copy-start.7
  348.1 2.5 copy-start.6
  350.6 175.2 %reduce-scatter.11.cloned.1.call-start = ((), (), s32[]{:S(2)}) async-start(), calls=%async_computation.11 | async-start | bytes 1081344 | tf_op jit(solution)/shard_map/reduce_scatter | solution.py:100
  356.8 2.7 copy-start.8
  359.2 208.7 %reduce-scatter.7.cloned.1.call-start = ((), (), s32[]{:S(2)}) async-start(), calls=%async_computation.9 | async-start | bytes 2359296 | tf_op jit(solution)/shard_map/reduce_scatter | solution.py:107
  382.0 185.9 %copy-start.13 = (f32[2048]{0:T(1024)S(1)}, f32[2048]{0:T(1024)}, u32[]{:S(2)}) copy-start(f32[2048]{0:T(1024)} %param.10) | copy-start | bytes 24580
  382.0 187.0 %copy-start.10 = (bf16[64,2048]{1,0:T(8,128)(2,1)S(1)}, bf16[64,2048]{1,0:T(8,128)(2,1)}, u32[]{:S(2)}) copy-start(bf16[64,2048]{1,0:T(8,128)(2,1)} %param.16) | copy-start | bytes 786436
Sparse Core Ops, SparseCore 0:
  10.5 51.7 all-gather.6
  64.8 46.9 all-gather.8
  114.2 35.7 all-gather.4
  178.8 41.1 reduce-scatter.4
  302.6 33.0 all-gather.10
  350.7 86.3 reduce-scatter.8
  440.9 84.8 reduce-scatter.10
  528.4 39.4 reduce-scatter.6
where the time goes:
time: 583 us; the launch traced here: 578 us
  waiting for transfers between devices  393 us (67%)
  blocking collectives  79 us (14%)
  local copies, waits for them, and re-layouts  41 us (7%)
  matrix products  38.3 us (7%)
  between operations  14.4 us (2%)
  other arithmetic  11 us (2%)
    reduce_scatter x1, waiting for transfers between devices, on_device(): lax.psum_scatter(arrange(out_terms).astype(jnp.bfloat16), 'tok', scatter_...  87.3 us
    psum x1, blocking collectives, on_device(): lax.psum((score_sums, token_counts), ('tok', 'feat'))  79 us
    reduce_scatter x1, waiting for transfers between devices, on_device(): lax.psum_scatter(arrange(in_terms).astype(jnp.bfloat16), 'tok', scatter_d...  55.1 us
    all_gather x1, waiting for transfers between devices, on_device(): lax.all_gather(w_in, 'tok', axis=0, tiled=True)  50.6 us
    all_gather x1, waiting for transfers between devices, on_device(): lax.all_gather(w_out, 'tok', axis=0, tiled=True)  48.1 us
    reduce_scatter x1, waiting for transfers between devices, on_device(): lax.psum_scatter(spread(back_terms).astype(jnp.bfloat16), 'feat', scatter...  40.7 us
    reduce_scatter x1, waiting for transfers between devices, on_device(): lax.psum_scatter(spread(out_terms_fwd).astype(jnp.bfloat16), 'feat', scat...  40.6 us
    all_gather x1, waiting for transfers between devices, on_device(): normed_rows = lax.all_gather(normed, 'feat', axis=0, tiled=True)  36.6 us
  transfers between devices with their start and end apart: 8, of which 8 were waited for; matrix products, arithmetic and copies ran while one was open for 7% of the time, Pallas kernels for 0%

commit v1 on v0

v1 whole, which is shorter than its diff:
```python
import functools
import heapq
import math

import jax
import jax.numpy as jnp
from jax import lax
from jax.experimental import pallas as pl
from jax.experimental.pallas import tpu as pltpu
from jax.sharding import PartitionSpec as P

BLK = 128
EPS = 1e-06
LOSS_WEIGHT = 8.0
X, Y, C, Z = 4, 4, 2, 8
Q = Y * C
ROWS = 64
WIDTH = 2048
KB = 4
MESH = pl.DeviceIdType.MESH
F32, BF16 = jnp.float32, jnp.bfloat16
NT = (((1,), (1,)), ((), ()))
NN = (((1,), (0,)), ((), ()))
VM = pl.BlockSpec(memory_space=pltpu.VMEM)
ANY = pl.BlockSpec(memory_space=pl.ANY)


def dot(a, b, dims):
    return lax.dot_general(a, b, dims, preferred_element_type=F32)


class Place:
    def __init__(self):
        t = lax.axis_index("tok")
        self.z = lax.axis_index("feat")
        self.t = t
        self.q = lax.rem(t, Q)
        self.c = lax.rem(t, C)
        self.y = lax.rem(t // C, Y)
        self.x = t // Q

    def at(self, x=None, y=None, c=None, z=None):
        x, y = self.x if x is None else x, self.y if y is None else y
        c, z = self.c if c is None else c, self.z if z is None else z
        return {"tok": (x * Y + y) * C + c, "feat": z}

    def sibling(self):
        return self.at(c=1 - self.c)

    def along(self, axis, by):
        n = {"x": X, "y": Y, "z": Z}[axis]
        me = {"x": self.x, "y": self.y, "z": self.z}[axis]
        return self.at(**{axis: lax.rem(me + by + n, n)})

    def member(self, by):
        return {"tok": self.x * Q + lax.rem(self.q + by + Q, Q), "feat": self.z}

    def flat(self, by):
        n = X * Q * Z
        d = lax.rem(self.t * Z + self.z + by + n, n)
        return {"tok": d // Z, "feat": lax.rem(d, Z)}


class Mail:
    def __init__(self, send_sem, recv_sem):
        self.send_sem, self.recv_sem, self.sent = send_sem, recv_sem, []

    def send(self, src, dst, to):
        i = len(self.sent)
        copy = pltpu.make_async_remote_copy(
            src_ref=src,
            dst_ref=dst,
            send_sem=self.send_sem.at[i],
            recv_sem=self.recv_sem.at[i],
            device_id=to,
            device_id_type=MESH,
        )
        copy.start()
        self.sent.append(copy)
        return copy

    def close(self):
        for copy in self.sent:
            copy.wait_send()


def greet(devices):
    barrier = pltpu.get_barrier_semaphore()
    for device in devices:
        pl.semaphore_signal(barrier, inc=1, device_id=device, device_id_type=MESH)
    pl.semaphore_wait(barrier, len(devices))


class Flows:
    def __init__(self):
        self.heap, self.now, self.count = [], 0.0, 0

    def add(self, flow):
        heapq.heappush(self.heap, (self.now, self.count, flow))
        self.count += 1

    def run(self):
        while self.heap:
            self.now, _, flow = heapq.heappop(self.heap)
            for delay in flow:
                heapq.heappush(self.heap, (self.now + delay, self.count, flow))
                self.count += 1
                break


def gather_ring(mail, n, me, plus, minus, piece, half, delays, arrived=None):
    a = mail.send(piece(me), piece(me), plus)
    b = mail.send(piece(me), piece(me), minus)
    for step in range(1, n // 2 + 1):
        yield delays[step - 1]
        last = step == n // 2
        a.wait_recv()
        left = lax.rem(me - step + n, n)
        if not last:
            ref = half(left, 0) if step == n // 2 - 1 else piece(left)
            a = mail.send(ref, ref, plus)
            if arrived:
                arrived(left, None)
        elif arrived:
            arrived(left, 0)
        b.wait_recv()
        right = lax.rem(me + step, n)
        if not last:
            ref = half(right, 1) if step == n // 2 - 1 else piece(right)
            b = mail.send(ref, ref, minus)
            if arrived:
                arrived(right, None)
        elif arrived:
            arrived(right, 1)


def reduce_ring(mail, n, me, plus, minus, own, half, full, stage, land, delays, done):
    steps = n // 2
    far = lax.rem(me + steps, n)
    a = mail.send(half(own(far), 0), half(land(0, 1), 0), plus)
    b = mail.send(half(own(far), 1), half(land(1, 1), 1), minus)
    for step in range(2, steps + 1):
        yield delays[step - 2]
        for way in (0, 1):
            (a, b)[way].wait_recv()
            dest = lax.rem(me + steps - step + 1, n) if way == 0 else lax.rem(me - steps + step - 1 + n, n)
            mine, came, out = own(dest), land(way, step - 1), stage(way, step)
            if step == 2:
                half(out, way)[...] = (half(mine, way)[...].astype(F32) + half(came, way)[...].astype(F32)).astype(BF16)
                half(out, 1 - way)[...] = half(mine, 1 - way)[...]
            else:
                out[...] = (mine[...].astype(F32) + came[...].astype(F32)).astype(BF16)
            sent = mail.send(out, land(way, step), plus if way == 0 else minus)
            if way == 0:
                a = sent
            else:
                b = sent
    yield delays[steps - 1]
    a.wait_recv()
    b.wait_recv()
    done(own(me)[...].astype(F32) + land(0, steps)[...].astype(F32) + land(1, steps)[...].astype(F32))


def gather_kernel(x_ref, up_ref, gain_ref, win_ref, wout_ref, bi_ref,
                  nrm_all, up_all, win_all, wout_all, bi_all,
                  nrm_v, send_sem, recv_sem, local_sem):
    p = Place()
    mail = Mail(send_sem, recv_sem)
    ring = [p.along(a, s) for a in "xz" for s in (-1, 1)]
    greet([p.member(o) for o in range(1, Q)] + ring[:2] + [p.along("z", o) for o in range(1, Z)])
    local = []

    def keep(src, dst):
        copy = pltpu.make_async_copy(src, dst, local_sem.at[len(local)])
        copy.start()
        local.append(copy)

    flows = Flows()

    def columns(ref, q):
        return ref.at[:, pl.ds(pl.multiple_of(q * BLK, BLK), BLK)]

    def my_rows(ref):
        return ref.at[pl.ds(pl.multiple_of(p.q * 16, 16), 16), :]

    in_slab, out_slab = win_all.at[p.z, p.x], wout_all.at[p.x, p.z]
    deals = []
    for o in range(1, Q):
        to, q = p.member(o), lax.rem(p.q + o, Q)
        deals.append(mail.send(columns(win_ref, q), my_rows(in_slab), to))
        deals.append(mail.send(columns(wout_ref, q), my_rows(out_slab), to))
    keep(columns(win_ref, p.q), my_rows(in_slab))
    keep(columns(wout_ref, p.q), my_rows(out_slab))
    slab_copies = list(local)
    tables = [mail.send(bi_ref, bi_all.at[p.z], p.along("z", o)) for o in range(1, Z)]
    keep(bi_ref, bi_all.at[p.z])

    def tokens(own, out, first):
        def piece(y):
            return out.at[y * C + p.c]

        def half(y, h):
            return out.at[y * C + p.c, pl.ds(h * 32, 32), :]

        relays = []

        def arrived(y, h):
            ref = piece(y) if h is None else half(y, h)
            relays.append(mail.send(ref, ref, p.sibling()))

        plus, minus = p.along("y", 1), p.along("y", -1)
        mine = out.at[p.q]
        a = mail.send(own, mine, plus)
        b = mail.send(own, mine, minus)
        relays.append(mail.send(own, mine, p.sibling()))
        keep(own, mine)
        yield first
        left, right = lax.rem(p.y + 3, Y), lax.rem(p.y + 1, Y)
        a.wait_recv()
        a = mail.send(half(left, 0), half(left, 0), plus)
        arrived(left, None)
        b.wait_recv()
        b = mail.send(half(right, 1), half(right, 1), minus)
        arrived(right, None)
        yield 5.0
        far = lax.rem(p.y + 2, Y)
        a.wait_recv()
        arrived(far, 0)
        b.wait_recv()
        arrived(far, 1)
        yield 5.0
        for copy in relays:
            copy.wait_recv()

    flows.add(tokens(up_ref, up_all, 10.0))
    xf = x_ref[...].astype(F32)
    inv = lax.rsqrt(jnp.mean(xf * xf, axis=1, keepdims=True) + EPS)
    nrm_v[...] = (xf * inv * gain_ref[...]).astype(BF16)
    flows.add(tokens(nrm_v, nrm_all, 9.5))

    xplus, xminus = p.along("x", 1), p.along("x", -1)
    zplus, zminus = p.along("z", 1), p.along("z", -1)
    slow, quick = [2.5] * 4, [2.0] * 4

    def w_in_z(k):
        return gather_ring(
            mail, Z, p.z, zplus, zminus,
            lambda z: win_all.at[z, k],
            lambda z, h: win_all.at[z, k, pl.ds(h * 64, 64), :],
            [3.5] * 4)

    def w_out_x(z):
        return gather_ring(
            mail, X, p.x, xplus, xminus,
            lambda x: wout_all.at[x, z],
            lambda x, h: wout_all.at[x, z, pl.ds(h * 64, 64), :],
            [3.5] * 4)

    def weights():
        yield 2.5
        for copy in deals:
            copy.wait_recv()
        for copy in slab_copies:
            copy.wait()

        parts = {}

        def got(x, h):
            if h is None:
                flows.add(w_in_z(x))
            else:
                parts[h] = True
                if len(parts) == 2:
                    flows.add(w_in_z(x))

        both = {}

        def got_out(z, h):
            if h is None:
                flows.add(w_out_x(z))
            else:
                both[h] = True
                if len(both) == 2:
                    flows.add(w_out_x(z))

        flows.add(gather_ring(
            mail, X, p.x, xplus, xminus,
            lambda x: win_all.at[p.z, x],
            lambda x, h: win_all.at[p.z, x, pl.ds(h * 64, 64), :],
            quick, got))
        flows.add(gather_ring(
            mail, Z, p.z, zplus, zminus,
            lambda z: wout_all.at[p.x, z],
            lambda z, h: wout_all.at[p.x, z, pl.ds(h * 64, 64), :],
            quick, got_out))
        flows.add(w_in_z(p.x))
        flows.add(w_out_x(p.z))

    flows.add(weights())
    flows.run()
    for copy in tables:
        copy.wait_recv()
    for copy in local[len(slab_copies):]:
        copy.wait()
    mail.close()


def gather_all(x, up, gain, w_in, w_out, table):
    return pl.pallas_call(
        gather_kernel,
        name="gather_all",
        out_shape=(
            jax.ShapeDtypeStruct((Q, ROWS, WIDTH), BF16),
            jax.ShapeDtypeStruct((Q, ROWS, WIDTH), BF16),
            jax.ShapeDtypeStruct((Z, KB, BLK, BLK), BF16),
            jax.ShapeDtypeStruct((KB, Z, BLK, BLK), BF16),
            jax.ShapeDtypeStruct((Z, 8, BLK), jnp.int32),
        ),
        in_specs=[VM] * 6,
        out_specs=(ANY,) * 5,
        scratch_shapes=[
            pltpu.VMEM((ROWS, WIDTH), BF16),
            pltpu.SemaphoreType.DMA((128,)),
            pltpu.SemaphoreType.DMA((128,)),
            pltpu.SemaphoreType.DMA((8,)),
        ],
        compiler_params=pltpu.CompilerParams(collective_id=0, has_side_effects=True),
    )(x, up, gain, w_in, w_out, table)


SQ = math.sqrt(2.0 / math.pi)


def forward_kernel(bi_ref, nrm_ref, win_ref, wout_ref, part_ref, act_ref, slope_ref, acc):
    q = lax.rem(lax.axis_index("tok"), Q)
    acc[...] = jnp.zeros_like(acc)

    def block(j, carry):
        at = [pl.multiple_of(bi_ref[j, q, k] * BLK, BLK) for k in range(KB)]
        picked = jnp.concatenate([nrm_ref[:, pl.ds(a, BLK)] for a in at], axis=1)
        v = dot(picked, win_ref[j].reshape(KB * BLK, BLK), NN)
        tanh = jnp.tanh(SQ * (v + 0.044715 * (v * v * v)))
        act = 0.5 * v * (1.0 + tanh)
        slope = 0.5 * (1.0 + tanh) + 0.5 * v * (1.0 - tanh * tanh) * (SQ * (1.0 + 3.0 * 0.044715 * (v * v)))
        act_half = act.astype(BF16)
        act_ref[j] = act.T.astype(BF16)
        slope_ref[j] = slope
        for k in range(KB):
            acc[:, pl.ds(at[k], BLK)] += dot(act_half, wout_ref[k, j], NT)
        return carry

    lax.fori_loop(0, Z, block, 0)
    part_ref[...] = acc[...].astype(BF16)


def forward(table, nrm, w_in, w_out):
    n = Q * ROWS
    return pl.pallas_call(
        forward_kernel,
        name="forward",
        out_shape=(
            jax.ShapeDtypeStruct((n, WIDTH), BF16),
            jax.ShapeDtypeStruct((Z, BLK, n), BF16),
            jax.ShapeDtypeStruct((Z, n, BLK), F32),
        ),
        in_specs=[pl.BlockSpec(memory_space=pltpu.SMEM), VM, VM, VM],
        out_specs=(VM,) * 3,
        scratch_shapes=[pltpu.VMEM((n, WIDTH), F32)],
    )(table, nrm, w_in, w_out)


def halves(ref, h):
    return ref.at[pl.ds(h * 32, 32), :]


def reduce_tokens(mail, p, part, rs, pair, stage, land, done, times):
    other = 1 - p.c
    order = [2, 1, 3, 0]
    sends = {}
    for o in order:
        y = lax.rem(p.y + o, Y)
        sends[o] = mail.send(part.at[y * C + other], rs.at[y], p.sibling())
    yield times[0]

    def fold(o):
        y = lax.rem(p.y + o, Y)
        sends[o].wait_recv()
        pair[y] = (part[y * C + p.c].astype(F32) + rs[y].astype(F32)).astype(BF16)

    fold(2)
    plus, minus = p.along("y", 1), p.along("y", -1)
    flow = reduce_ring(
        mail, Y, p.y, plus, minus,
        lambda y: pair.at[y], halves, None,
        lambda way, step: stage.at[way],
        lambda way, step: land.at[way, step - 1],
        times[1:], done)
    delay = next(flow)
    fold(1)
    fold(3)
    fold(0)
    yield delay
    yield from flow


def branch_kernel(part_ref, x_ref, seg_ref, teacher_ref, readout_ref,
                  lo_ref, coeff_ref,
                  rs, pair, stage, land, ids, scores, send_sem, recv_sem):
    p = Place()
    mail = Mail(send_sem, recv_sem)
    near = [p.flat(1), p.flat(-1)]
    greet([p.member(o) for o in range(1, Q)] + near)
    ids[0] = seg_ref[...]
    id_copies = [mail.send(ids.at[0], ids.at[1 + i], near[i]) for i in (0, 1)]
    total = []
    flows = Flows()
    flows.add(reduce_tokens(mail, p, part_ref, rs, pair, stage, land, total.append, [1.0, 4.0, 4.0]))
    eye = lax.broadcasted_iota(jnp.int32, (ROWS, BLK), 0) == lax.broadcasted_iota(jnp.int32, (ROWS, BLK), 1)
    ids_col = jnp.sum(jnp.where(eye, seg_ref[0:1, :], 0.0), axis=1, keepdims=True)
    segs = teacher_ref.shape[1]
    hot = lax.broadcasted_iota(jnp.int32, (ROWS, segs), 1).astype(F32) == ids_col
    teacher = jnp.sum(jnp.where(hot, teacher_ref[...], 0.0), axis=1, keepdims=True)
    flows.run()
    lo = (x_ref[...].astype(F32) + total[0]).astype(BF16)
    lo_ref[...] = lo
    score = jnp.sum(lo.astype(F32) * readout_ref[...], axis=1, keepdims=True)
    score_row = jnp.sum(jnp.where(eye, score, 0.0), axis=0, keepdims=True)
    scores[0] = jnp.broadcast_to(score_row, (8, BLK))
    copies = [mail.send(scores.at[0], scores.at[1 + i], near[i]) for i in (0, 1)]
    for copy in id_copies + copies:
        copy.wait_recv()
    sums = jnp.zeros((ROWS, 1), F32)
    counts = jnp.zeros((ROWS, 1), F32)
    for i in range(3):
        same = ids[i, 0:1, :] == ids_col
        sums += jnp.sum(jnp.where(same, scores[i, 0:1, :], 0.0), axis=1, keepdims=True)
        counts += jnp.sum(jnp.where(same, 1.0, 0.0), axis=1, keepdims=True)
    coeff = (2.0 * LOSS_WEIGHT) * (sums / counts - teacher)
    coeff_row = jnp.sum(jnp.where(eye, coeff, 0.0), axis=0, keepdims=True)
    coeff_ref[p.q] = jnp.broadcast_to(coeff_row, (8, BLK))
    out = [mail.send(coeff_ref.at[p.q], coeff_ref.at[p.q], p.member(o)) for o in range(1, Q)]
    for copy in out:
        copy.wait_recv()
    mail.close()


def branch_sum(part, x, seg, teacher, readout):
    return pl.pallas_call(
        branch_kernel,
        name="branch_sum",
        out_shape=(
            jax.ShapeDtypeStruct((ROWS, WIDTH), BF16),
            jax.ShapeDtypeStruct((Q, 8, BLK), F32),
        ),
        in_specs=[VM] * 5,
        out_specs=(VM,) * 2,
        scratch_shapes=[
            pltpu.VMEM((Y, ROWS, WIDTH), BF16),
            pltpu.VMEM((Y, ROWS, WIDTH), BF16),
            pltpu.VMEM((2, ROWS, WIDTH), BF16),
            pltpu.VMEM((2, 2, ROWS, WIDTH), BF16),
            pltpu.VMEM((3, 8, BLK), F32),
            pltpu.VMEM((3, 8, BLK), F32),
            pltpu.SemaphoreType.DMA((32,)),
            pltpu.SemaphoreType.DMA((32,)),
        ],
        compiler_params=pltpu.CompilerParams(collective_id=1, has_side_effects=True),
    )(part, x, seg, teacher, readout)


def backward_kernel(bi_ref, up_ref, coeff_ref, readout_ref, nrm_ref, win_ref, wout_ref, act_ref, slope_ref,
                    back_ref, din_ref, dout_ref, cot, acc):
    q = lax.rem(lax.axis_index("tok"), Q)
    acc[...] = jnp.zeros_like(acc)
    eye = lax.broadcasted_iota(jnp.int32, (ROWS, BLK), 0) == lax.broadcasted_iota(jnp.int32, (ROWS, BLK), 1)

    def form(b, carry):
        rows = pl.ds(pl.multiple_of(b * ROWS, ROWS), ROWS)
        coeff = jnp.sum(jnp.where(eye, coeff_ref[b][0:1, :], 0.0), axis=1, keepdims=True)
        cot[rows, :] = (up_ref[rows, :].astype(F32) + coeff * readout_ref[...]).astype(BF16)
        return carry

    lax.fori_loop(0, Q, form, 0)

    def block(j, carry):
        at = [pl.multiple_of(bi_ref[j, q, k] * BLK, BLK) for k in range(KB)]
        picked = jnp.concatenate([cot[:, pl.ds(a, BLK)] for a in at], axis=1)
        w_out = jnp.concatenate([wout_ref[k, j] for k in range(KB)], axis=0)
        upper = dot(picked, w_out, NN)
        pre = upper * slope_ref[j]
        pre_half = pre.astype(BF16)
        pre_t = pre.T.astype(BF16)
        act_t = act_ref[j]
        for k in range(KB):
            cols = pl.ds(at[k], BLK)
            acc[:, cols] += dot(pre_half, win_ref[j, k], NT)
            din_ref[j, k] = dot(pre_t, nrm_ref[:, cols], NN).astype(BF16)
            dout_ref[k, j] = dot(act_t, cot[:, cols], NN).astype(BF16)
        return carry

    lax.fori_loop(0, Z, block, 0)
    back_ref[...] = acc[...].astype(BF16)


def backward(table, up, coeff, readout, nrm, w_in, w_out, act, slope):
    n = Q * ROWS
    return pl.pallas_call(
        backward_kernel,
        name="backward",
        out_shape=(
            jax.ShapeDtypeStruct((n, WIDTH), BF16),
            jax.ShapeDtypeStruct((Z, KB, BLK, BLK), BF16),
            jax.ShapeDtypeStruct((KB, Z, BLK, BLK), BF16),
        ),
        in_specs=[pl.BlockSpec(memory_space=pltpu.SMEM)] + [VM] * 8,
        out_specs=(VM,) * 3,
        scratch_shapes=[pltpu.VMEM((n, WIDTH), BF16), pltpu.VMEM((n, WIDTH), F32)],
    )(table, up, coeff, readout, nrm, w_in, w_out, act, slope)


def rows64(ref, h):
    return ref.at[pl.ds(h * 64, 64), :]


def finish_kernel(scale, back_ref, din_ref, dout_ref, x_ref, up_ref, coeff_ref, readout_ref, gain_ref,
                  ig_ref, gin_ref, gout_ref,
                  rs, pair, stage, land,
                  za_stage, za_land, za_sum, xa_stage, xa_land,
                  xb_stage, xb_land, xb_sum, zb_stage, zb_land,
                  slab, dealt, send_sem, recv_sem):
    p = Place()
    mail = Mail(send_sem, recv_sem)
    greet([p.member(o) for o in range(1, Q)] + [p.along(a, s) for a in "xz" for s in (-1, 1)])
    flows = Flows()
    total = []
    flows.add(reduce_tokens(mail, p, back_ref, rs, pair, stage, land, total.append, [1.0, 8.0, 8.0]))
    xplus, xminus = p.along("x", 1), p.along("x", -1)
    zplus, zminus = p.along("z", 1), p.along("z", -1)
    deals = []

    def deal(w):
        def done(value):
            slab[w] = (value * scale).T.astype(BF16)
            dealt[w, p.q] = slab[w, pl.ds(pl.multiple_of(p.q * 16, 16), 16), :]
            for o in range(1, Q):
                q = lax.rem(p.q + o, Q)
                rows = slab.at[w, pl.ds(pl.multiple_of(q * 16, 16), 16), :]
                deals.append(mail.send(rows, dealt.at[w, p.q], p.member(o)))
        return done

    left = [KB]

    def in_z(k):
        def done(value):
            za_sum[k] = value.astype(BF16)
            left[0] -= 1
            if left[0] == 0:
                flows.add(reduce_ring(
                    mail, X, p.x, xplus, xminus,
                    lambda x: za_sum.at[x], rows64, None,
                    lambda way, step: xa_stage.at[way], lambda way, step: xa_land.at[way, step - 1],
                    [2.0] * 4, deal(0)))
        return reduce_ring(
            mail, Z, p.z, zplus, zminus,
            lambda z: din_ref.at[z, k], rows64, None,
            lambda way, step: za_stage.at[k, way, step - 2], lambda way, step: za_land.at[k, way, step - 1],
            [3.0] * 4, done)

    rest = [Z]

    def out_x(z):
        def done(value):
            xb_sum[z] = value.astype(BF16)
            rest[0] -= 1
            if rest[0] == 0:
                flows.add(reduce_ring(
                    mail, Z, p.z, zplus, zminus,
                    lambda z: xb_sum.at[z], rows64, None,
                    lambda way, step: zb_stage.at[way, step - 2], lambda way, step: zb_land.at[way, step - 1],
                    [2.0] * 4, deal(1)))
        return reduce_ring(
            mail, X, p.x, xplus, xminus,
            lambda x: dout_ref.at[x, z], rows64, None,
            lambda way, step: xb_stage.at[z, way], lambda way, step: xb_land.at[z, way, step - 1],
            [5.0] * 4, done)

    for i in range(KB):
        flows.add(in_z(i))
        flows.add(out_x(2 * i))
        flows.add(out_x(2 * i + 1))
    flows.run()

    xf = x_ref[...].astype(F32)
    inv = lax.rsqrt(jnp.mean(xf * xf, axis=1, keepdims=True) + EPS)
    eye = lax.broadcasted_iota(jnp.int32, (ROWS, BLK), 0) == lax.broadcasted_iota(jnp.int32, (ROWS, BLK), 1)
    coeff = jnp.sum(jnp.where(eye, coeff_ref[p.q][0:1, :], 0.0), axis=1, keepdims=True)
    cot = (up_ref[...].astype(F32) + coeff * readout_ref[...]).astype(BF16).astype(F32)
    scaled = total[0] * gain_ref[...]
    inner = jnp.mean(scaled * xf, axis=1, keepdims=True)
    ig_ref[...] = (cot + (inv * scaled - xf * (inv * inv * inv) * inner)).astype(BF16)
    for copy in deals:
        copy.wait_recv()
    for q in range(Q):
        gin_ref[:, q * BLK:(q + 1) * BLK] = dealt[0, q].astype(F32)
        gout_ref[:, q * BLK:(q + 1) * BLK] = dealt[1, q].astype(F32)
    mail.close()


def finish(scale, back, din, dout, x, up, coeff, readout, gain):
    tile = (BLK, BLK)
    return pl.pallas_call(
        functools.partial(finish_kernel, scale),
        name="finish",
        out_shape=(
            jax.ShapeDtypeStruct((ROWS, WIDTH), BF16),
            jax.ShapeDtypeStruct((16, Q * BLK), F32),
            jax.ShapeDtypeStruct((16, Q * BLK), F32),
        ),
        in_specs=[VM] * 8,
        out_specs=(VM,) * 3,
        scratch_shapes=[
            pltpu.VMEM((Y, ROWS, WIDTH), BF16),
            pltpu.VMEM((Y, ROWS, WIDTH), BF16),
            pltpu.VMEM((2, ROWS, WIDTH), BF16),
            pltpu.VMEM((2, 2, ROWS, WIDTH), BF16),
            pltpu.VMEM((KB, 2, 3) + tile, BF16),
            pltpu.VMEM((KB, 2, 4) + tile, BF16),
            pltpu.VMEM((KB,) + tile, BF16),
            pltpu.VMEM((2,) + tile, BF16),
            pltpu.VMEM((2, 2) + tile, BF16),
            pltpu.VMEM((Z, 2) + tile, BF16),
            pltpu.VMEM((Z, 2, 2) + tile, BF16),
            pltpu.VMEM((Z,) + tile, BF16),
            pltpu.VMEM((2, 3) + tile, BF16),
            pltpu.VMEM((2, 4) + tile, BF16),
            pltpu.VMEM((2,) + tile, BF16),
            pltpu.VMEM((2, Q, 16, BLK), BF16),
            pltpu.SemaphoreType.DMA((112,)),
            pltpu.SemaphoreType.DMA((112,)),
        ],
        compiler_params=pltpu.CompilerParams(collective_id=2, has_side_effects=True),
    )(back, din, dout, x, up, coeff, readout, gain)


def on_device(
    inputs, norm_gain, w_in, w_out, block_index, segment_ids, teacher_scores, upstream, readout
):
    scale = 1.0 / math.sqrt(ROWS * X * Q * Z)
    gain, head, teacher = norm_gain[None, :], readout[None, :], teacher_scores[None, :]
    table = jnp.pad(block_index, ((0, 0), (0, BLK - KB)))
    seg = jnp.pad(segment_ids.astype(F32), (0, BLK - ROWS), constant_values=-1.0)
    seg = jnp.broadcast_to(seg[None, :], (8, BLK))
    nrm_all, up_all, win_all, wout_all, bi_all = gather_all(inputs, upstream, gain, w_in, w_out, table)
    nrm = nrm_all.reshape(Q * ROWS, WIDTH)
    part, act, slope = forward(bi_all, nrm, win_all, wout_all)
    layer_out, coeff = branch_sum(part.reshape(Q, ROWS, WIDTH), inputs, seg, teacher, head)
    back, din, dout = backward(
        bi_all, up_all.reshape(Q * ROWS, WIDTH), coeff, head, nrm, win_all, wout_all, act, slope)
    input_grad, grad_in, grad_out = finish(
        scale, back.reshape(Q, ROWS, WIDTH), din, dout, inputs, upstream, coeff, head, gain)
    return layer_out, input_grad, grad_in, grad_out


def solution(mesh):
    return jax.shard_map(
        on_device,
        mesh=mesh,
        in_specs=(
            P(("tok", "feat"), None),
            P(),
            P("tok", "feat"),
            P("tok", "feat"),
            P("feat", None),
            P(("tok", "feat")),
            P(),
            P(("tok", "feat"), None),
            P(),
        ),
        out_specs=(
            P(("tok", "feat"), None),
            P(("tok", "feat"), None),
            P("tok", "feat"),
            P("tok", "feat"),
        ),
        check_vma=False,
    )
```

time: 583 us -> 139 us (0.24)
  waiting for transfers between devices: 393 us -> 0 us
  Pallas kernels: 0 us -> 131 us
  blocking collectives: 79 us -> 0 us
  matrix products: 38.3 us -> 0 us
  local copies, waits for them, and re-layouts: 41 us -> 7.28 us
  between operations: 14.4 us -> 0.69 us
  other arithmetic: 11 us -> 0.01 us
    reduce_scatter x4 -> x0, waiting for transfers between devices: 224 us -> none  [the longest x1 87.3 us: on_device(): lax.psum_scatter(arrange(out_terms).astype(jnp.bfloat16), 'tok', scatter_...]
    all_gather x4 -> x0, waiting for transfers between devices: 168 us -> none  [the longest x1 50.6 us: on_device(): lax.all_gather(w_in, 'tok', axis=0, tiled=True)]
    pallas_call x0 -> x5, Pallas kernels: none -> 131 us  [the longest x1 38.3 us: gather_all(): pl.pallas_call(gather_kernel, name='gather_all', out_shape=(jax.ShapeDtyp...]
    psum x1 -> x0, blocking collectives: 79 us -> none  [on_device(): lax.psum((score_sums, token_counts), ('tok', 'feat'))]
    dot_general x12 -> x0, matrix products: 38.3 us -> none  [the longest x2 11.2 us: spread(): jnp.einsum('rjkc,jkd->rdc', grouped, sel_wide, precision=lax.Precision.HI...]
    reshape x2 -> x0, local copies, waits for them, and re-layouts: 20.9 us -> none  [spread(): grouped = terms.reshape(group_rows, blocks_here, per_hidden, BLK)]
    convert_element_type x6 -> x1, other arithmetic: 8.4 us -> 0.01 us  [on_device(): segment_ids.astype(F32)]
    convert_element_type x4 -> x0, local copies, waits for them, and re-layouts: 6.23 us -> none  [the longest x1 2.42 us: on_device(): arrange(in_terms).astype(jnp.bfloat16)]
  transfers between devices with their start and end apart: 8 -> 0, of which waited for: 8 -> 0; matrix products, arithmetic and copies ran while one was open for 7% -> 0% of each run, Pallas kernels for 0% -> 0%
where the time goes in v1:
time: 139 us
  Pallas kernels  131 us (94%)
  local copies, waits for them, and re-layouts  7.28 us (5%)
    pallas_call x1, Pallas kernels, gather_all(): pl.pallas_call(gather_kernel, name='gather_all', out_shape=(jax.ShapeDtyp...  38.3 us
    pallas_call x1, Pallas kernels, finish(): pl.pallas_call(functools.partial(finish_kernel, scale), name='finish', ou...  35.6 us
    pallas_call x1, Pallas kernels, branch_sum(): pl.pallas_call(branch_kernel, name='branch_sum', out_shape=(jax.ShapeDtyp...  29.3 us
    pallas_call x1, Pallas kernels, backward(): pl.pallas_call(backward_kernel, name='backward', out_shape=(jax.ShapeDtyp...  16.5 us
    pallas_call x1, Pallas kernels, forward(): pl.pallas_call(forward_kernel, name='forward', out_shape=(jax.ShapeDtypeS...  11.1 us
    unnamed x9, local copies, waits for them, and re-layouts  6.09 us

profile of v1, /device:TPU:1, one launch (start us, length us, event | category | flops | bytes accessed | tf_op | source)
XLA Modules:
  0.0 138.8 jit_solution(9016475027554870403)
XLA Ops:
  0.6 0.8 copy.13
  1.4 0.6 pad.8.bi_ref
  2.0 38.3 %gather_all.1 = (bf16[8,64,2048]{2,1,0:T(8,128)(2,1)}, bf16[8,64,2048]{2,1,0:T(8,128)(2,1)}, bf16[8,4,128,128]{3,2,1,0:T(8,128)(2,1)}, bf16[4,8,128,128]{3,2,1,0:T(8,128)(2,1)}, s32[8,8,128]{2,1,0:T(8,128)}) custom-call(bf16[64,2048]{1,0:T(8,128)(2,1)} %x_ref.5, bf16[64,2048]{1,0:T(8,128)(2,1)} %up_ref.3, f32[1,2048]{1,0:T(1,128)} %bitcast.15, ...), custom_call_target="tpu_custom_call" | custom-call | tf_op jit(solution)/shard_map/gather_all/pallas_call | solution.py:309
  40.3 0.0 copy-start.1
  40.3 11.1 %forward.1 = (bf16[512,2048]{1,0:T(8,128)(2,1)}, bf16[8,128,512]{2,1,0:T(8,128)(2,1)}, f32[8,512,128]{2,1,0:T(8,128)}) custom-call(s32[8,8,128]{2,1,0:T(8,128)} %get-tuple-element.20.bi_ref, bf16[512,2048]{1,0:T(8,128)(2,1)} %bitcast.7, bf16[8,4,128,128]{3,2,1,0:T(8,128)(2,1)} %get-tuple-element.22.win_ref, bf16[4,8,128,128]{3,2,1,0:T(8,128)(2,1)} %get-tuple-element.23.wout_ref), custom_call_target="tpu_custom_call" | custom-call | tf_op jit(solution)/shard_map/forward/pallas_call | solution.py:358
  51.4 0.0 copy-done.1
  51.4 0.6 broadcast_in_dim.16.seg_ref
  52.0 29.3 %branch_sum.1 = (bf16[64,2048]{1,0:T(8,128)(2,1)}, f32[8,8,128]{2,1,0:T(8,128)}) custom-call(bf16[8,64,2048]{2,1,0:T(8,128)(2,1)} %bitcast.10, bf16[64,2048]{1,0:T(8,128)(2,1)} %x_ref.5, f32[8,128]{1,0:T(8,128)} %broadcast_in_dim.16.seg_ref, f32[1,1024]{1,0:T(1,128)} %bitcast.17, f32[1,2048]{1,0:T(1,128)} %bitcast.12), custom_call_target="tpu_custom_call" | custom-call | tf_op jit(solution)/shard_map/branch_sum/pallas_call | solution.py:448
  81.3 16.5 %backward.1 = (bf16[512,2048]{1,0:T(8,128)(2,1)}, bf16[8,4,128,128]{3,2,1,0:T(8,128)(2,1)}, bf16[4,8,128,128]{3,2,1,0:T(8,128)(2,1)}) custom-call(s32[8,8,128]{2,1,0:T(8,128)} %get-tuple-element.20.bi_ref, bf16[512,2048]{1,0:T(8,128)(2,1)} %bitcast.11, f32[8,8,128]{2,1,0:T(8,128)} %get-tuple-element.27.coeff_ref, f32[1,2048]{1,0:T(1,128)} %bitcast.13, ...), custom_call_target="tpu_custom_call" | custom-call | tf_op jit(solution)/shard_map/backward/pallas_call | solution.py:507
  97.8 0.0 copy-start
  97.8 35.6 %finish.1 = (bf16[64,2048]{1,0:T(8,128)(2,1)}, f32[16,1024]{1,0:T(8,128)}, f32[16,1024]{1,0:T(8,128)}) custom-call(bf16[8,64,2048]{2,1,0:T(8,128)(2,1)} %bitcast.9, bf16[8,4,128,128]{3,2,1,0:T(8,128)(2,1)} %get-tuple-element.31.din_ref, bf16[4,8,128,128]{3,2,1,0:T(8,128)(2,1)} %get-tuple-element.32.dout_ref, bf16[64,2048]{1,0:T(8,128)(2,1)} %x_ref.5, ...), custom_call_target="tpu_custom_call" | custom-call | tf_op jit(solution)/shard_map/finish/pallas_call | solution.py:611
  133.4 0.0 copy-done
  133.4 0.7 copy.18
  134.2 1.7 %copy.19 = bf16[64,2048]{1,0:T(8,128)(2,1)} copy(bf16[64,2048]{1,0:T(8,128)(2,1)} %get-tuple-element.41) | data formatting | bytes 524288
  135.8 1.5 %copy.20 = f32[16,1024]{1,0:T(8,128)} copy(f32[16,1024]{1,0:T(8,128)} %get-tuple-element.42) | data formatting | bytes 131072
  137.3 1.5 %copy.21 = f32[16,1024]{1,0:T(8,128)} copy(f32[16,1024]{1,0:T(8,128)} %get-tuple-element.43) | data formatting | bytes 131072
  (2 shorter events, 0.0 us)
Async XLA Ops:
  40.3 11.1 %copy-start.1 = (s32[64]{0:T(128)S(1)}, s32[64]{0:T(128)}, u32[]{:S(2)}) copy-start(s32[64]{0:T(128)} %param.14) | copy-start | bytes 772
  97.8 35.7 %copy-start = (bf16[64,2048]{1,0:T(8,128)(2,1)S(1)}, bf16[64,2048]{1,0:T(8,128)(2,1)}, u32[]{:S(2)}) copy-start(bf16[64,2048]{1,0:T(8,128)(2,1)} %get-tuple-element.40) | copy-start | bytes 786436

commit v2 on v1

v2 whole, which is shorter than its diff:
```python
import functools
import heapq
import math

import jax
import jax.numpy as jnp
from jax import lax
from jax.experimental import pallas as pl
from jax.experimental.pallas import tpu as pltpu
from jax.sharding import PartitionSpec as P

BLK = 128
EPS = 1e-06
LOSS_WEIGHT = 8.0
X, Y, C, Z = 4, 4, 2, 8
Q = Y * C
ROWS = 64
WIDTH = 2048
KB = 4
MESH = pl.DeviceIdType.MESH
F32, BF16 = jnp.float32, jnp.bfloat16
NT = (((1,), (1,)), ((), ()))
NN = (((1,), (0,)), ((), ()))
VM = pl.BlockSpec(memory_space=pltpu.VMEM)
ANY = pl.BlockSpec(memory_space=pl.ANY)


def dot(a, b, dims):
    return lax.dot_general(a, b, dims, preferred_element_type=F32)


class Place:
    def __init__(self):
        t = lax.axis_index("tok")
        self.z = lax.axis_index("feat")
        self.t = t
        self.q = lax.rem(t, Q)
        self.c = lax.rem(t, C)
        self.y = lax.rem(t // C, Y)
        self.x = t // Q

    def at(self, x=None, y=None, c=None, z=None):
        x, y = self.x if x is None else x, self.y if y is None else y
        c, z = self.c if c is None else c, self.z if z is None else z
        return {"tok": (x * Y + y) * C + c, "feat": z}

    def sibling(self):
        return self.at(c=1 - self.c)

    def along(self, axis, by):
        n = {"x": X, "y": Y, "z": Z}[axis]
        me = {"x": self.x, "y": self.y, "z": self.z}[axis]
        return self.at(**{axis: lax.rem(me + by + n, n)})

    def member(self, by):
        return {"tok": self.x * Q + lax.rem(self.q + by + Q, Q), "feat": self.z}

    def plane(self, dx, by):
        return {"tok": lax.rem(self.x + dx + X, X) * Q + lax.rem(self.q + by + Q, Q), "feat": self.z}

    def flat(self, by):
        n = X * Q * Z
        d = lax.rem(self.t * Z + self.z + by + n, n)
        return {"tok": d // Z, "feat": lax.rem(d, Z)}


class Mail:
    def __init__(self, send_sem, recv_sem):
        self.send_sem, self.recv_sem, self.sent = send_sem, recv_sem, []

    def send(self, src, dst, to):
        i = len(self.sent)
        copy = pltpu.make_async_remote_copy(
            src_ref=src,
            dst_ref=dst,
            send_sem=self.send_sem.at[i],
            recv_sem=self.recv_sem.at[i],
            device_id=to,
            device_id_type=MESH,
        )
        copy.start()
        self.sent.append(copy)
        return copy

    def close(self):
        for copy in self.sent:
            copy.wait_send()


def greet(devices, meanwhile=None):
    barrier = pltpu.get_barrier_semaphore()
    for device in devices:
        pl.semaphore_signal(barrier, inc=1, device_id=device, device_id_type=MESH)
    if meanwhile:
        meanwhile()
    pl.semaphore_wait(barrier, len(devices))


class Flows:
    def __init__(self):
        self.heap, self.now, self.count = [], 0.0, 0

    def add(self, flow):
        heapq.heappush(self.heap, (self.now, self.count, flow))
        self.count += 1

    def run(self):
        while self.heap:
            self.now, _, flow = heapq.heappop(self.heap)
            for delay in flow:
                heapq.heappush(self.heap, (self.now + delay, self.count, flow))
                self.count += 1
                break


def gather_ring(mail, n, me, plus, minus, piece, half, delays, arrived=None):
    a = mail.send(piece(me), piece(me), plus)
    b = mail.send(piece(me), piece(me), minus)
    for step in range(1, n // 2 + 1):
        yield delays[step - 1]
        last = step == n // 2
        a.wait_recv()
        left = lax.rem(me - step + n, n)
        if not last:
            ref = half(left, 0) if step == n // 2 - 1 else piece(left)
            a = mail.send(ref, ref, plus)
            if arrived:
                arrived(left, None)
        elif arrived:
            arrived(left, 0)
        b.wait_recv()
        right = lax.rem(me + step, n)
        if not last:
            ref = half(right, 1) if step == n // 2 - 1 else piece(right)
            b = mail.send(ref, ref, minus)
            if arrived:
                arrived(right, None)
        elif arrived:
            arrived(right, 1)


def reduce_ring(mail, n, plus, minus, own, half, stage, land, delays, done):
    steps = n // 2
    a = mail.send(half(own(steps), 0), half(land(0, 1), 0), plus)
    b = mail.send(half(own(steps), 1), half(land(1, 1), 1), minus)
    for step in range(2, steps + 1):
        yield delays[step - 2]
        for way in (0, 1):
            mine = own(steps - step + 1 if way == 0 else n - steps + step - 1)
            (a, b)[way].wait_recv()
            came, out = land(way, step - 1), stage(way, step)
            if step == 2:
                half(out, way)[...] = (half(mine, way)[...].astype(F32) + half(came, way)[...].astype(F32)).astype(BF16)
                half(out, 1 - way)[...] = half(mine, 1 - way)[...]
            else:
                out[...] = (mine[...].astype(F32) + came[...].astype(F32)).astype(BF16)
            sent = mail.send(out, land(way, step), minus if way else plus)
            if way == 0:
                a = sent
            else:
                b = sent
    yield delays[steps - 1]
    mine = own(0)
    a.wait_recv()
    b.wait_recv()
    done(mine[...].astype(F32) + land(0, steps)[...].astype(F32) + land(1, steps)[...].astype(F32))


def gather_kernel(x_ref, up_ref, gain_ref, win_ref, wout_ref, bi_ref,
                  nrm_all, up_all, win_all, wout_all, bi_all,
                  x_v, gain_v, nrm_v, send_sem, recv_sem, local_sem):
    p = Place()
    mail = Mail(send_sem, recv_sem)
    local = []

    def keep(src, dst):
        copy = pltpu.make_async_copy(src, dst, local_sem.at[len(local)])
        copy.start()
        local.append(copy)
        return copy

    loads = [keep(x_ref, x_v), keep(gain_ref, gain_v)]
    greet([p.plane(dx, o) for dx in range(X) for o in range(Q) if dx or o] + [p.along("z", s) for s in (-1, 1)])
    flows = Flows()
    yplus, yminus = p.along("y", 1), p.along("y", -1)
    zplus, zminus = p.along("z", 1), p.along("z", -1)

    def columns(ref, q):
        return ref.at[:, pl.ds(pl.multiple_of(q * BLK, BLK), BLK)]

    def my_rows(ref):
        return ref.at[pl.ds(pl.multiple_of(p.q * 16, 16), 16), :]

    in_slab, out_slab = win_all.at[p.z, p.x], wout_all.at[p.x, p.z]
    in_deals, out_deals = {}, []
    for o in range(Q):
        q = lax.rem(p.q + o, Q)
        for dx in range(X):
            if dx or o:
                in_deals[dx, o] = mail.send(columns(win_ref, q), my_rows(in_slab), p.plane(dx, o))
        if o:
            out_deals.append(mail.send(columns(wout_ref, q), my_rows(out_slab), p.member(o)))
    slab_copies = [keep(columns(win_ref, p.q), my_rows(in_slab)), keep(columns(wout_ref, p.q), my_rows(out_slab))]

    def tokens(own, out, first):
        def half(y, h):
            return out.at[y * C + p.c, pl.ds(h * 32, 32), :]

        def mine(h):
            return own.at[pl.ds(h * 32, 32), :]

        relays = []

        def pass_on(ref, to):
            relays.append(mail.send(ref, ref, to))
            return relays[-1]

        a0 = mail.send(mine(0), half(p.y, 0), yplus)
        b1 = mail.send(mine(1), half(p.y, 1), yminus)
        a1 = mail.send(mine(1), half(p.y, 1), yplus)
        b0 = mail.send(mine(0), half(p.y, 0), yminus)
        relays.append(mail.send(own, out.at[p.q], p.sibling()))
        keep(own, out.at[p.q])
        left, right, far = lax.rem(p.y + 3, Y), lax.rem(p.y + 1, Y), lax.rem(p.y + 2, Y)
        yield first
        a0.wait_recv()
        fa = mail.send(half(left, 0), half(left, 0), yplus)
        pass_on(half(left, 0), p.sibling())
        b1.wait_recv()
        fb = mail.send(half(right, 1), half(right, 1), yminus)
        pass_on(half(right, 1), p.sibling())
        yield 3.0
        a1.wait_recv()
        pass_on(half(left, 1), p.sibling())
        b0.wait_recv()
        pass_on(half(right, 0), p.sibling())
        yield 8.3
        fa.wait_recv()
        pass_on(half(far, 0), p.sibling())
        fb.wait_recv()
        pass_on(half(far, 1), p.sibling())
        yield 2.0
        for copy in relays:
            copy.wait_recv()

    def table():
        mine = bi_all.at[p.z]
        keep(bi_ref, mine)
        a = mail.send(bi_ref, mine, zplus)
        b = mail.send(bi_ref, mine, zminus)
        for step in range(1, Z // 2 + 1):
            yield 2.5
            a.wait_recv()
            left = bi_all.at[lax.rem(p.z - step + Z, Z)]
            if step < Z // 2:
                a = mail.send(left, left, zplus)
                b.wait_recv()
                right = bi_all.at[lax.rem(p.z + step, Z)]
                if step < Z // 2 - 1:
                    b = mail.send(right, right, zminus)

    flows.add(tokens(up_ref, up_all, 4.5))
    flows.add(table())
    quick = [2.5] * 4

    def w_in_z(k):
        return gather_ring(
            mail, Z, p.z, zplus, zminus,
            lambda z: win_all.at[z, k],
            lambda z, h: win_all.at[z, k, pl.ds(h * 64, 64), :],
            [3.0] * 4)

    def w_out_x(z):
        ref = wout_all.at[p.x, z]
        copies = [mail.send(ref, ref, p.along("x", dx)) for dx in (1, 2, 3)]
        yield 6.0
        for copy in copies:
            copy.wait_recv()

    def w_in():
        yield 2.5
        slab_copies[0].wait()
        for dx in range(X):
            for o in range(Q):
                if dx or o:
                    in_deals[dx, o].wait_recv()
            flows.add(w_in_z(lax.rem(p.x - dx + X, X)))
            yield 0.3

    def w_out():
        yield 2.6
        slab_copies[1].wait()
        for copy in out_deals:
            copy.wait_recv()
        seen = []

        def got(z, h):
            if h is not None:
                seen.append(h)
            if h is None or len(seen) == 2:
                flows.add(w_out_x(z))

        flows.add(gather_ring(
            mail, Z, p.z, zplus, zminus,
            lambda z: wout_all.at[p.x, z],
            lambda z, h: wout_all.at[p.x, z, pl.ds(h * 64, 64), :],
            quick, got))
        flows.add(w_out_x(p.z))

    flows.add(w_in())
    flows.add(w_out())

    def normed():
        for copy in loads:
            copy.wait()
        xf = x_v[...].astype(F32)
        inv = lax.rsqrt(jnp.mean(xf * xf, axis=1, keepdims=True) + EPS)
        nrm_v[...] = (xf * inv * gain_v[...]).astype(BF16)
        yield from tokens(nrm_v, nrm_all, 10.0)

    flows.add(normed())
    flows.run()
    for copy in local[4:]:
        copy.wait()
    mail.close()


def gather_all(x, up, gain, w_in, w_out, table):
    far = pl.BlockSpec(memory_space=pltpu.HBM)
    return pl.pallas_call(
        gather_kernel,
        name="gather_all",
        out_shape=(
            jax.ShapeDtypeStruct((Q, ROWS, WIDTH), BF16),
            jax.ShapeDtypeStruct((Q, ROWS, WIDTH), BF16),
            jax.ShapeDtypeStruct((Z, KB, BLK, BLK), BF16),
            jax.ShapeDtypeStruct((KB, Z, BLK, BLK), BF16),
            jax.ShapeDtypeStruct((Z, KB, Z), jnp.int32),
        ),
        in_specs=[far] * 6,
        out_specs=(ANY,) * 5,
        scratch_shapes=[
            pltpu.VMEM((ROWS, WIDTH), BF16),
            pltpu.VMEM((1, WIDTH), F32),
            pltpu.VMEM((ROWS, WIDTH), BF16),
            pltpu.SemaphoreType.DMA((136,)),
            pltpu.SemaphoreType.DMA((136,)),
            pltpu.SemaphoreType.DMA((8,)),
        ],
        compiler_params=pltpu.CompilerParams(collective_id=0, has_side_effects=True, vmem_limit_bytes=4 << 20),
    )(x, up, gain, w_in, w_out, table)


SQ = math.sqrt(2.0 / math.pi)
UNROLL = 8


def forward_kernel(bi_ref, nrm_ref, win_ref, wout_ref, part_ref, act_ref, slope_ref, wide_ref, blocks_ref, acc):
    q = lax.rem(lax.axis_index("tok"), Q)
    acc[...] = jnp.zeros_like(acc)
    wide_ref[...] = jnp.zeros_like(wide_ref)
    for d in range(WIDTH // BLK):
        blocks_ref[d] = nrm_ref[:, d * BLK:(d + 1) * BLK]

    def block(j, carry):
        at = [pl.multiple_of(bi_ref[j, k, q] * BLK, BLK) for k in range(KB)]
        for k in range(KB):
            wide_ref[pl.ds(at[k], BLK), pl.ds(pl.multiple_of(j * BLK, BLK), BLK)] = win_ref[j, k]
        picked = jnp.concatenate([nrm_ref[:, pl.ds(a, BLK)] for a in at], axis=1)
        v = dot(picked, win_ref[j].reshape(KB * BLK, BLK), NN)
        tanh = jnp.tanh(SQ * (v + 0.044715 * (v * v * v)))
        act = 0.5 * v * (1.0 + tanh)
        slope = 0.5 * (1.0 + tanh) + 0.5 * v * (1.0 - tanh * tanh) * (SQ * (1.0 + 3.0 * 0.044715 * (v * v)))
        act_half = act.astype(BF16)
        act_ref[j] = act.T.astype(BF16)
        slope_ref[j] = slope
        w_out = jnp.concatenate([wout_ref[k, j] for k in range(KB)], axis=0)
        terms = dot(act_half, w_out, NT)
        for k in range(KB):
            acc[:, pl.ds(at[k], BLK)] += terms[:, k * BLK:(k + 1) * BLK]
        return carry

    lax.fori_loop(0, Z, block, 0, unroll=UNROLL)
    part_ref[...] = acc[...].astype(BF16)


def forward(table, nrm, w_in, w_out):
    n = Q * ROWS
    return pl.pallas_call(
        forward_kernel,
        name="forward",
        out_shape=(
            jax.ShapeDtypeStruct((n, WIDTH), BF16),
            jax.ShapeDtypeStruct((Z, BLK, n), BF16),
            jax.ShapeDtypeStruct((Z, n, BLK), F32),
            jax.ShapeDtypeStruct((WIDTH, Z * BLK), BF16),
            jax.ShapeDtypeStruct((WIDTH // BLK, n, BLK), BF16),
        ),
        in_specs=[pl.BlockSpec(memory_space=pltpu.SMEM), VM, VM, VM],
        out_specs=(VM,) * 5,
        scratch_shapes=[pltpu.VMEM((n, WIDTH), F32)],
        compiler_params=pltpu.CompilerParams(vmem_limit_bytes=20<<20),
    )(table, nrm, w_in, w_out)


def halves(ref, h):
    return ref.at[pl.ds(h * 32, 32), :]


def reduce_tokens(mail, p, part, rs, pair, stage, land, done, times):
    other = 1 - p.c
    sends = {}
    ys = [lax.rem(p.y + o, Y) for o in range(Y)]
    for o in (2, 1, 3, 0):
        sends[o] = mail.send(part(ys[o] * C + other), rs.at[ys[o]], p.sibling())
    plus, minus = p.along("y", 1), p.along("y", -1)
    yield times[0]

    def fold(o):
        sends[o].wait_recv()
        pair[ys[o]] = (part(ys[o] * C + p.c)[...].astype(F32) + rs[ys[o]].astype(F32)).astype(BF16)

    fold(2)
    a = mail.send(halves(pair.at[ys[2]], 0), land.at[0, 0], plus)
    b = mail.send(halves(pair.at[ys[2]], 1), land.at[1, 0], minus)
    fold(1)
    a1 = mail.send(halves(pair.at[ys[1]], 1), land.at[0, 1], plus)
    fold(3)
    b1 = mail.send(halves(pair.at[ys[3]], 0), land.at[1, 1], minus)
    fold(0)
    yield times[1]
    a.wait_recv()
    stage[0] = (pair[ys[1], 0:32].astype(F32) + land[0, 0].astype(F32)).astype(BF16)
    a2 = mail.send(stage.at[0], land.at[0, 2], plus)
    b.wait_recv()
    stage[1] = (pair[ys[3], 32:64].astype(F32) + land[1, 0].astype(F32)).astype(BF16)
    b2 = mail.send(stage.at[1], land.at[1, 2], minus)
    yield times[2]
    for copy in (a1, b1, a2, b2):
        copy.wait_recv()
    top = pair[ys[0], 0:32].astype(F32) + land[0, 2].astype(F32) + land[1, 1].astype(F32)
    low = pair[ys[0], 32:64].astype(F32) + land[0, 1].astype(F32) + land[1, 2].astype(F32)
    done(jnp.concatenate([top, low], axis=0))


def branch_kernel(part_ref, x_ref, seg_ref, teacher_ref, readout_ref,
                  lo_ref, coeff_ref,
                  rs, pair, stage, land, ids, scores, send_sem, recv_sem):
    p = Place()
    mail = Mail(send_sem, recv_sem)
    near = [p.flat(1), p.flat(-1)]
    greet([p.member(o) for o in range(1, Q)] + near)
    ids[0] = jnp.full((8, BLK), -1.0, F32)
    ids[0, 0:1, 0:ROWS] = seg_ref[...].astype(F32)
    id_copies = [mail.send(ids.at[0], ids.at[1 + i], near[i]) for i in (0, 1)]
    total = []
    flows = Flows()
    flows.add(reduce_tokens(mail, p, lambda q: part_ref.at[q], rs, pair, stage, land, total.append, [1.0, 4.0, 4.0]))
    eye = lax.broadcasted_iota(jnp.int32, (ROWS, BLK), 0) == lax.broadcasted_iota(jnp.int32, (ROWS, BLK), 1)
    ids_col = jnp.sum(jnp.where(eye, ids[0, 0:1, :], 0.0), axis=1, keepdims=True)
    segs = teacher_ref.shape[1]
    hot = lax.broadcasted_iota(jnp.int32, (ROWS, segs), 1).astype(F32) == ids_col
    teacher = jnp.sum(jnp.where(hot, teacher_ref[...], 0.0), axis=1, keepdims=True)
    flows.run()
    lo = (x_ref[...].astype(F32) + total[0]).astype(BF16)
    lo_ref[...] = lo
    score = jnp.sum(lo.astype(F32) * readout_ref[...], axis=1, keepdims=True)
    score_row = jnp.sum(jnp.where(eye, score, 0.0), axis=0, keepdims=True)
    scores[0] = jnp.broadcast_to(score_row, (8, BLK))
    copies = [mail.send(scores.at[0], scores.at[1 + i], near[i]) for i in (0, 1)]
    for copy in id_copies + copies:
        copy.wait_recv()
    sums = jnp.zeros((ROWS, 1), F32)
    counts = jnp.zeros((ROWS, 1), F32)
    for i in range(3):
        same = ids[i, 0:1, :] == ids_col
        sums += jnp.sum(jnp.where(same, scores[i, 0:1, :], 0.0), axis=1, keepdims=True)
        counts += jnp.sum(jnp.where(same, 1.0, 0.0), axis=1, keepdims=True)
    coeff = (2.0 * LOSS_WEIGHT) * (sums / counts - teacher)
    coeff_row = jnp.sum(jnp.where(eye, coeff, 0.0), axis=0, keepdims=True)
    coeff_ref[p.q] = jnp.broadcast_to(coeff_row, (8, BLK))
    out = [mail.send(coeff_ref.at[p.q], coeff_ref.at[p.q], p.member(o)) for o in range(1, Q)]
    for copy in out:
        copy.wait_recv()
    mail.close()


def branch_sum(part, x, seg, teacher, readout):
    return pl.pallas_call(
        branch_kernel,
        name="branch_sum",
        out_shape=(
            jax.ShapeDtypeStruct((ROWS, WIDTH), BF16),
            jax.ShapeDtypeStruct((Q, 8, BLK), F32),
        ),
        in_specs=[VM] * 5,
        out_specs=(VM,) * 2,
        scratch_shapes=[
            pltpu.VMEM((Y, ROWS, WIDTH), BF16),
            pltpu.VMEM((Y, ROWS, WIDTH), BF16),
            pltpu.VMEM((2, ROWS // 2, WIDTH), BF16),
            pltpu.VMEM((2, 3, ROWS // 2, WIDTH), BF16),
            pltpu.VMEM((3, 8, BLK), F32),
            pltpu.VMEM((3, 8, BLK), F32),
            pltpu.SemaphoreType.DMA((32,)),
            pltpu.SemaphoreType.DMA((32,)),
        ],
        compiler_params=pltpu.CompilerParams(collective_id=1, has_side_effects=True, vmem_limit_bytes=12<<20),
    )(part, x, seg, teacher, readout)


def rows64(ref, h):
    return ref.at[pl.ds(h * 64, 64), :]


FAR_FIRST = (4, 3, 5, 2, 6, 1, 7, 0)


def backward_kernel(scale, bi_ref, up_all, coeff_ref, readout_ref, nrm_ref, wout_ref, act_ref, slope_ref, wide_ref,
                    x_ref, up_ref, gain_ref,
                    ig_ref, gin_ref, gout_ref,
                    cot, pre, back, din, dout,
                    rs, pair, stage, land,
                    za_stage, za_land, za_sum,
                    xb_land, xb_sum, zb_stage, zb_land,
                    slab, dealt_in, dealt, send_sem, recv_sem):
    p = Place()
    mail = Mail(send_sem, recv_sem)
    eye = lax.broadcasted_iota(jnp.int32, (ROWS, BLK), 0) == lax.broadcasted_iota(jnp.int32, (ROWS, BLK), 1)

    def form():
        for b in range(Q):
            rows = slice(b * ROWS, (b + 1) * ROWS)
            coeff = jnp.sum(jnp.where(eye, coeff_ref[b, 0:1, :], 0.0), axis=1, keepdims=True)
            value = (up_all[rows, :].astype(F32) + coeff * readout_ref[...]).astype(BF16)
            for d in range(WIDTH // BLK):
                cot[d, rows, :] = value[:, d * BLK:(d + 1) * BLK]

    def block(dz):
        j = lax.rem(p.z + dz, Z)
        at = [bi_ref[j, k, p.q] for k in range(KB)]
        picked = jnp.concatenate([cot[a] for a in at], axis=1)
        chosen = jnp.concatenate([nrm_ref[a] for a in at], axis=1)
        w_out = jnp.concatenate([wout_ref[k, j] for k in range(KB)], axis=0)
        value = dot(picked, w_out, NN) * slope_ref[j]
        pre[:, pl.ds(pl.multiple_of(j * BLK, BLK), BLK)] = value.astype(BF16)
        d_in = (dot(value.T.astype(BF16), chosen, NN) * scale).astype(BF16)
        d_out = (dot(act_ref[j], picked, NN) * scale).astype(BF16)
        for k in range(KB):
            cols = slice(k * BLK, (k + 1) * BLK)
            din[dz, k] = d_in[:, cols]
            dout[dz, k] = d_out[:, cols]

    def first():
        form()
        block(FAR_FIRST[0])

    greet([p.plane(dx, o) for dx in range(X) for o in range(Q) if dx or o] + [p.along("z", s) for s in (-1, 1)], first)
    zplus, zminus = p.along("z", 1), p.along("z", -1)
    flows = Flows()
    ready = {FAR_FIRST[0]}
    total, deals, x_sends = [], [], {}

    def out_x(dz):
        for dx in (1, 2, 3):
            x = lax.rem(p.x + dx, X)
            x_sends[dz, dx] = mail.send(dout.at[dz, x], xb_land.at[dx - 1, dz], p.along("x", dx))

    def in_z(dx):
        k = lax.rem(p.x + dx, X)

        def own(dz):
            assert dz in ready
            return din.at[dz, k]

        def done(value):
            za_sum[dx] = value.T.astype(BF16)
            for o in range(Q):
                rows = pl.ds(pl.multiple_of(lax.rem(p.q + o, Q) * 16, 16), 16)
                if dx == 0 and o == 0:
                    dealt_in[p.x, p.q] = za_sum[dx, rows, :]
                else:
                    deals.append(mail.send(za_sum.at[dx, rows, :], dealt_in.at[p.x, p.q], p.plane(dx, o)))

        return reduce_ring(
            mail, Z, zplus, zminus, own, rows64,
            lambda way, step: za_stage.at[dx, way, step - 2], lambda way, step: za_land.at[dx, way, step - 1],
            [3.2] * 4, done)

    summed = set()

    def out_own(dz):
        if dz not in summed:
            assert dz in ready
            summed.add(dz)
            for dx in (1, 2, 3):
                x_sends[dz, dx].wait_recv()
            value = dout[dz, p.x].astype(F32) + sum(xb_land[i, dz].astype(F32) for i in range(3))
            xb_sum[dz] = value.astype(BF16)
        return xb_sum.at[dz]

    def deal(value):
        slab[...] = value.T.astype(BF16)
        dealt[p.q] = slab[pl.ds(pl.multiple_of(p.q * 16, 16), 16), :]
        for o in range(1, Q):
            rows = slab.at[pl.ds(pl.multiple_of(lax.rem(p.q + o, Q) * 16, 16), 16), :]
            deals.append(mail.send(rows, dealt.at[p.q], p.member(o)))

    def out_z():
        yield 3.5
        yield from reduce_ring(
            mail, Z, zplus, zminus, out_own, rows64,
            lambda way, step: zb_stage.at[way, step - 2], lambda way, step: zb_land.at[way, step - 1],
            [3.0, 3.0, 3.0, 3.0], deal)

    def compute():
        out_x(FAR_FIRST[0])
        for dz in FAR_FIRST[1:]:
            block(dz)
            ready.add(dz)
            out_x(dz)
            yield 1.0
        for n in range(4):
            cols = slice(n * 512, (n + 1) * 512)
            back[:, cols] = dot(pre[...], wide_ref[cols, :], NT).astype(BF16)
        flows.add(reduce_tokens(
            mail, p, lambda q: back.at[pl.ds(pl.multiple_of(q * ROWS, ROWS), ROWS), :],
            rs, pair, stage, land, total.append, [1.0, 5.0, 6.0]))

    for dx in (1, 2, 3, 0):
        flows.add(in_z(dx))
    flows.add(compute())
    flows.add(out_z())
    flows.run()

    xf = x_ref[...].astype(F32)
    inv = lax.rsqrt(jnp.mean(xf * xf, axis=1, keepdims=True) + EPS)
    coeff = jnp.sum(jnp.where(eye, coeff_ref[p.q][0:1, :], 0.0), axis=1, keepdims=True)
    own_cot = (up_ref[...].astype(F32) + coeff * readout_ref[...]).astype(BF16).astype(F32)
    scaled = total[0] * gain_ref[...]
    inner = jnp.mean(scaled * xf, axis=1, keepdims=True)
    ig_ref[...] = (own_cot + (inv * scaled - xf * (inv * inv * inv) * inner)).astype(BF16)
    for copy in deals:
        copy.wait_recv()
    for q in range(Q):
        cols = slice(q * BLK, (q + 1) * BLK)
        gin_ref[:, cols] = sum(dealt_in[x, q].astype(F32) for x in range(X))
        gout_ref[:, cols] = dealt[q].astype(F32)
    mail.close()


def backward(scale, table, up_all, coeff, readout, nrm, w_out, act, slope, wide, x, up, gain):
    n = Q * ROWS
    tile = (BLK, BLK)
    return pl.pallas_call(
        functools.partial(backward_kernel, scale),
        name="backward",
        out_shape=(
            jax.ShapeDtypeStruct((ROWS, WIDTH), BF16),
            jax.ShapeDtypeStruct((16, Q * BLK), F32),
            jax.ShapeDtypeStruct((16, Q * BLK), F32),
        ),
        in_specs=[pl.BlockSpec(memory_space=pltpu.SMEM)] + [VM] * 11,
        out_specs=(VM,) * 3,
        scratch_shapes=[
            pltpu.VMEM((WIDTH // BLK, n, BLK), BF16),
            pltpu.VMEM((n, Z * BLK), BF16),
            pltpu.VMEM((n, WIDTH), BF16),
            pltpu.VMEM((Z, KB) + tile, BF16),
            pltpu.VMEM((Z, KB) + tile, BF16),
            pltpu.VMEM((Y, ROWS, WIDTH), BF16),
            pltpu.VMEM((Y, ROWS, WIDTH), BF16),
            pltpu.VMEM((2, ROWS // 2, WIDTH), BF16),
            pltpu.VMEM((2, 3, ROWS // 2, WIDTH), BF16),
            pltpu.VMEM((KB, 2, 3) + tile, BF16),
            pltpu.VMEM((KB, 2, 4) + tile, BF16),
            pltpu.VMEM((KB,) + tile, BF16),
            pltpu.VMEM((3, Z) + tile, BF16),
            pltpu.VMEM((Z,) + tile, BF16),
            pltpu.VMEM((2, 3) + tile, BF16),
            pltpu.VMEM((2, 4) + tile, BF16),
            pltpu.VMEM(tile, BF16),
            pltpu.VMEM((X, Q, 16, BLK), BF16),
            pltpu.VMEM((Q, 16, BLK), BF16),
            pltpu.SemaphoreType.DMA((128,)),
            pltpu.SemaphoreType.DMA((128,)),
        ],
        compiler_params=pltpu.CompilerParams(collective_id=2, has_side_effects=True, vmem_limit_bytes=36 << 20),
    )(table, up_all, coeff, readout, nrm, w_out, act, slope, wide, x, up, gain)


def on_device(
    inputs, norm_gain, w_in, w_out, block_index, segment_ids, teacher_scores, upstream, readout
):
    scale = 1.0 / math.sqrt(ROWS * X * Q * Z)
    gain, head, teacher = norm_gain[None, :], readout[None, :], teacher_scores[None, :]
    table = block_index.T
    seg = segment_ids[None, :]
    nrm_all, up_all, win_all, wout_all, bi_all = gather_all(
        *[pltpu.with_memory_space_constraint(a, pltpu.HBM) for a in (inputs, upstream, gain, w_in, w_out, table)])
    nrm = nrm_all.reshape(Q * ROWS, WIDTH)
    part, act, slope, wide, blocks = forward(bi_all, nrm, win_all, wout_all)
    layer_out, coeff = branch_sum(part.reshape(Q, ROWS, WIDTH), inputs, seg, teacher, head)
    input_grad, grad_in, grad_out = backward(
        scale, bi_all, up_all.reshape(Q * ROWS, WIDTH), coeff, head, blocks, wout_all, act, slope, wide,
        inputs, upstream, gain)
    return layer_out, input_grad, grad_in, grad_out


def solution(mesh):
    return jax.shard_map(
        on_device,
        mesh=mesh,
        in_specs=(
            P(("tok", "feat"), None),
            P(),
            P("tok", "feat"),
            P("tok", "feat"),
            P("feat", None),
            P(("tok", "feat")),
            P(),
            P(("tok", "feat"), None),
            P(),
        ),
        out_specs=(
            P(("tok", "feat"), None),
            P(("tok", "feat"), None),
            P("tok", "feat"),
            P("tok", "feat"),
        ),
        check_vma=False,
    )
```

time: 139 us -> 104 us (0.75)
  Pallas kernels: 131 us -> 100 us
  local copies, waits for them, and re-layouts: 7.28 us -> 2.7 us
    pallas_call x2 -> x1, Pallas kernels: 52.1 us -> 34 us  [backward(): pl.pallas_call(functools.partial(backward_kernel, scale), name='backward'...]
    pallas_call x1, Pallas kernels: 29.3 us -> 22.2 us  [branch_sum(): pl.pallas_call(branch_kernel, name='branch_sum', out_shape=(jax.ShapeDtyp...]
    pallas_call x1, Pallas kernels: 11.1 us -> 6.26 us  [forward(): pl.pallas_call(forward_kernel, name='forward', out_shape=(jax.ShapeDtypeS...]
    unnamed x9 -> x16, local copies, waits for them, and re-layouts: 6.09 us -> 2.7 us
where the time goes in v2:
time: 104 us
  Pallas kernels  100 us (96%)
  local copies, waits for them, and re-layouts  2.7 us (3%)
    pallas_call x1, Pallas kernels, gather_all(): pl.pallas_call(gather_kernel, name='gather_all', out_shape=(jax.ShapeDtyp...  37.7 us
    pallas_call x1, Pallas kernels, backward(): pl.pallas_call(functools.partial(backward_kernel, scale), name='backward'...  34 us
    pallas_call x1, Pallas kernels, branch_sum(): pl.pallas_call(branch_kernel, name='branch_sum', out_shape=(jax.ShapeDtyp...  22.2 us
    pallas_call x1, Pallas kernels, forward(): pl.pallas_call(forward_kernel, name='forward', out_shape=(jax.ShapeDtypeS...  6.26 us
    unnamed x16, local copies, waits for them, and re-layouts  2.7 us

profile of v2, /device:TPU:1, one launch (start us, length us, event | category | flops | bytes accessed | tf_op | source)
XLA Modules:
  0.0 103.7 jit_solution(15437140629588332610)
XLA Ops:
  0.6 37.7 %gather_all.1 = (bf16[8,64,2048]{2,1,0:T(8,128)(2,1)S(1)}, bf16[8,64,2048]{2,1,0:T(8,128)(2,1)S(1)}, bf16[8,4,128,128]{3,2,1,0:T(8,128)(2,1)S(1)}, bf16[4,8,128,128]{3,2,1,0:T(8,128)(2,1)S(1)}, s32[8,4,8]{2,1,0:T(4,128)S(1)}) custom-call(bf16[64,2048]{1,0:T(8,128)(2,1)} %x_ref.5, bf16[64,2048]{1,0:T(8,128)(2,1)} %up_ref.3, f32[1,2048]{1,0:T(1,128)} %bitcast.11, ...), custom_call_target="tpu_custom_call" | custom-call | tf_op jit(solution)/shard_map/gather_all/pallas_call | solution.py:330
  38.4 0.0 copy-start
  38.4 0.0 copy-start.3
  38.4 0.0 copy-start.4
  38.4 0.0 copy-start.5
  38.4 6.3 %forward.1 = (bf16[512,2048]{1,0:T(8,128)(2,1)S(1)}, bf16[8,128,512]{2,1,0:T(8,128)(2,1)S(1)}, f32[8,512,128]{2,1,0:T(8,128)S(1)}, bf16[2048,1024]{1,0:T(8,128)(2,1)S(1)}, bf16[16,512,128]{2,1,0:T(8,128)(2,1)S(1)}) custom-call(s32[8,4,8]{2,1,0:T(4,128)S(1)} %get-tuple-element.19.bi_ref, bf16[512,2048]{1,0:T(8,128)(2,1)S(1)} %bitcast.9, ...), custom_call_target="tpu_custom_call" | custom-call | tf_op jit(solution)/shard_map/forward/pallas_call | solution.py:389
  44.7 0.0 copy-start.1
  44.7 0.0 copy-start.2
  44.7 0.0 copy-done
  44.7 0.0 copy-done.3
  44.7 0.0 copy-done.4
  44.7 0.0 copy-done.5
  44.8 22.2 %branch_sum.1 = (bf16[64,2048]{1,0:T(8,128)(2,1)S(1)}, f32[8,8,128]{2,1,0:T(8,128)S(1)}) custom-call(bf16[8,64,2048]{2,1,0:T(8,128)(2,1)S(1)} %bitcast.10, bf16[64,2048]{1,0:T(8,128)(2,1)S(1)} %copy-done, s32[1,64]{1,0:T(1,128)S(1)} %bitcast.16, f32[1,1024]{1,0:T(1,128)S(1)} %bitcast.15, f32[1,2048]{1,0:T(1,128)S(1)} %bitcast.13), custom_call_target="tpu_custom_call" | custom-call | tf_op jit(solution)/shard_map/branch_sum/pallas_call | solution.py:489
  67.0 0.0 copy-done.1
  67.0 0.0 copy-done.2
  67.0 34.0 %backward.1 = (bf16[64,2048]{1,0:T(8,128)(2,1)S(1)}, f32[16,1024]{1,0:T(8,128)S(1)}, f32[16,1024]{1,0:T(8,128)S(1)}) custom-call(s32[8,4,8]{2,1,0:T(4,128)S(1)} %get-tuple-element.19.bi_ref, bf16[512,2048]{1,0:T(8,128)(2,1)S(1)} %bitcast.8, f32[8,8,128]{2,1,0:T(8,128)S(1)} %get-tuple-element.26.coeff_ref, f32[1,2048]{1,0:T(1,128)S(1)} %bitcast.14, ...), custom_call_target="tpu_custom_call" | custom-call | tf_op jit(solution)/shard_map/backward/pallas_call | solution.py:655
  101.0 0.7 copy.17
  101.7 0.7 copy.18
  102.4 0.6 copy.19
  103.1 0.6 copy.20
Async XLA Ops:
  38.4 6.3 %copy-start = (bf16[64,2048]{1,0:T(8,128)(2,1)S(1)}, bf16[64,2048]{1,0:T(8,128)(2,1)}, u32[]{:S(2)}) copy-start(bf16[64,2048]{1,0:T(8,128)(2,1)} %x_ref.5) | copy-start | bytes 786436
  38.4 6.3 %copy-start.3 = (f32[2048]{0:T(1024)S(1)}, f32[2048]{0:T(1024)}, u32[]{:S(2)}) copy-start(f32[2048]{0:T(1024)} %param.17) | copy-start | bytes 24580
  38.4 6.3 %copy-start.4 = (f32[1024]{0:T(1024)S(1)}, f32[1024]{0:T(1024)}, u32[]{:S(2)}) copy-start(f32[1024]{0:T(1024)} %param.15) | copy-start | bytes 12292
  38.4 6.3 %copy-start.5 = (s32[64]{0:T(128)S(1)}, s32[64]{0:T(128)}, u32[]{:S(2)}) copy-start(s32[64]{0:T(128)} %param.14) | copy-start | bytes 772
  44.7 22.3 %copy-start.1 = (bf16[64,2048]{1,0:T(8,128)(2,1)S(1)}, bf16[64,2048]{1,0:T(8,128)(2,1)}, u32[]{:S(2)}) copy-start(bf16[64,2048]{1,0:T(8,128)(2,1)} %up_ref.3) | copy-start | bytes 786436
  44.7 22.3 %copy-start.2 = (f32[2048]{0:T(1024)S(1)}, f32[2048]{0:T(1024)}, u32[]{:S(2)}) copy-start(f32[2048]{0:T(1024)} %param.10) | copy-start | bytes 24580

commit v3 on v0

v3 whole, which is shorter than its diff:
```python
import functools
import heapq
import math

import jax
import jax.numpy as jnp
from jax import lax
from jax.experimental import pallas as pl
from jax.experimental.pallas import tpu as pltpu
from jax.sharding import PartitionSpec as P

BLK = 128
EPS = 1e-06
LOSS_WEIGHT = 8.0
X, Y, C, Z = 4, 4, 2, 8
Q = Y * C
ROWS = 64
WIDTH = 2048
KB = 4
MESH = pl.DeviceIdType.MESH
F32, BF16 = jnp.float32, jnp.bfloat16
NT = (((1,), (1,)), ((), ()))
NN = (((1,), (0,)), ((), ()))
VM = pl.BlockSpec(memory_space=pltpu.VMEM)
ANY = pl.BlockSpec(memory_space=pl.ANY)


def dot(a, b, dims):
    return lax.dot_general(a, b, dims, preferred_element_type=F32)


class Place:
    def __init__(self):
        t = lax.axis_index("tok")
        self.z = lax.axis_index("feat")
        self.t = t
        self.q = lax.rem(t, Q)
        self.c = lax.rem(t, C)
        self.y = lax.rem(t // C, Y)
        self.x = t // Q

    def at(self, x=None, y=None, c=None, z=None):
        x, y = self.x if x is None else x, self.y if y is None else y
        c, z = self.c if c is None else c, self.z if z is None else z
        return {"tok": (x * Y + y) * C + c, "feat": z}

    def sibling(self):
        return self.at(c=1 - self.c)

    def along(self, axis, by):
        n = {"x": X, "y": Y, "z": Z}[axis]
        me = {"x": self.x, "y": self.y, "z": self.z}[axis]
        return self.at(**{axis: lax.rem(me + by + n, n)})

    def member(self, by):
        return {"tok": self.x * Q + lax.rem(self.q + by + Q, Q), "feat": self.z}

    def plane(self, dx, by):
        return {"tok": lax.rem(self.x + dx + X, X) * Q + lax.rem(self.q + by + Q, Q), "feat": self.z}

    def flat(self, by):
        n = X * Q * Z
        d = lax.rem(self.t * Z + self.z + by + n, n)
        return {"tok": d // Z, "feat": lax.rem(d, Z)}


class Mail:
    def __init__(self, send_sem, recv_sem):
        self.send_sem, self.recv_sem, self.sent = send_sem, recv_sem, []

    def send(self, src, dst, to):
        i = len(self.sent)
        copy = pltpu.make_async_remote_copy(
            src_ref=src,
            dst_ref=dst,
            send_sem=self.send_sem.at[i],
            recv_sem=self.recv_sem.at[i],
            device_id=to,
            device_id_type=MESH,
        )
        copy.start()
        self.sent.append(copy)
        return copy

    def close(self):
        for copy in self.sent:
            copy.wait_send()


def greet(devices, meanwhile=None):
    barrier = pltpu.get_barrier_semaphore()
    for device in devices:
        pl.semaphore_signal(barrier, inc=1, device_id=device, device_id_type=MESH)
    if meanwhile:
        meanwhile()
    pl.semaphore_wait(barrier, len(devices))


class Flows:
    def __init__(self):
        self.heap, self.now, self.count = [], 0.0, 0
        self.ended, self.pending = set(), []

    def add(self, flow, name=None):
        heapq.heappush(self.heap, (self.now, self.count, flow, name))
        self.count += 1

    def after(self, names, start):
        self.pending.append((set(names), start))

    def end(self, name):
        self.ended.add(name)
        for names, start in list(self.pending):
            if names <= self.ended:
                self.pending.remove((names, start))
                start()

    def run(self):
        while self.heap:
            self.now, _, flow, name = heapq.heappop(self.heap)
            for delay in flow:
                heapq.heappush(self.heap, (self.now + delay, self.count, flow, name))
                self.count += 1
                break
            else:
                if name is not None:
                    self.end(name)
        assert not self.pending


def gather_ring(mail, n, me, plus, minus, piece, half, delays, arrived=None):
    a = mail.send(piece(me), piece(me), plus)
    b = mail.send(piece(me), piece(me), minus)
    for step in range(1, n // 2 + 1):
        yield delays[step - 1]
        last = step == n // 2
        a.wait_recv()
        left = lax.rem(me - step + n, n)
        if not last:
            ref = half(left, 0) if step == n // 2 - 1 else piece(left)
            a = mail.send(ref, ref, plus)
            if arrived:
                arrived(left, None)
        elif arrived:
            arrived(left, 0)
        b.wait_recv()
        right = lax.rem(me + step, n)
        if not last:
            ref = half(right, 1) if step == n // 2 - 1 else piece(right)
            b = mail.send(ref, ref, minus)
            if arrived:
                arrived(right, None)
        elif arrived:
            arrived(right, 1)


def reduce_ring(mail, n, plus, minus, own, half, stage, land, delays, done):
    steps = n // 2
    a = mail.send(half(own(steps), 0), half(land(0, 1), 0), plus)
    b = mail.send(half(own(steps), 1), half(land(1, 1), 1), minus)
    for step in range(2, steps + 1):
        yield delays[step - 2]
        for way in (0, 1):
            mine = own(steps - step + 1 if way == 0 else n - steps + step - 1)
            (a, b)[way].wait_recv()
            came, out = land(way, step - 1), stage(way, step)
            if step == 2:
                half(out, way)[...] = (half(mine, way)[...].astype(F32) + half(came, way)[...].astype(F32)).astype(BF16)
                half(out, 1 - way)[...] = half(mine, 1 - way)[...]
            else:
                out[...] = (mine[...].astype(F32) + came[...].astype(F32)).astype(BF16)
            sent = mail.send(out, land(way, step), minus if way else plus)
            if way == 0:
                a = sent
            else:
                b = sent
    yield delays[steps - 1]
    mine = own(0)
    a.wait_recv()
    b.wait_recv()
    done(mine[...].astype(F32) + land(0, steps)[...].astype(F32) + land(1, steps)[...].astype(F32))


def halves(ref, h):
    return ref.at[pl.ds(h * 32, 32), :]


def reduce_tokens(mail, p, make, part, rs, pair, stage, land, done, times):
    other = 1 - p.c
    sends = {}
    ys = [lax.rem(p.y + o, Y) for o in range(Y)]
    for two in ((2, 1), (3, 0)):
        make([ys[o] for o in two])
        for o in two:
            sends[o] = mail.send(part(ys[o] * C + other), rs.at[ys[o]], p.sibling())
        yield 0.2
    plus, minus = p.along("y", 1), p.along("y", -1)
    yield times[0]

    def fold(o):
        sends[o].wait_recv()
        pair[ys[o]] = (part(ys[o] * C + p.c)[...].astype(F32) + rs[ys[o]].astype(F32)).astype(BF16)

    fold(2)
    a = mail.send(halves(pair.at[ys[2]], 0), land.at[0, 0], plus)
    b = mail.send(halves(pair.at[ys[2]], 1), land.at[1, 0], minus)
    fold(1)
    a1 = mail.send(halves(pair.at[ys[1]], 1), land.at[0, 1], plus)
    fold(3)
    b1 = mail.send(halves(pair.at[ys[3]], 0), land.at[1, 1], minus)
    fold(0)
    yield times[1]
    a.wait_recv()
    stage[0] = (pair[ys[1], 0:32].astype(F32) + land[0, 0].astype(F32)).astype(BF16)
    a2 = mail.send(stage.at[0], land.at[0, 2], plus)
    b.wait_recv()
    stage[1] = (pair[ys[3], 32:64].astype(F32) + land[1, 0].astype(F32)).astype(BF16)
    b2 = mail.send(stage.at[1], land.at[1, 2], minus)
    yield times[2]
    for copy in (a1, b1, a2, b2):
        copy.wait_recv()
    top = pair[ys[0], 0:32].astype(F32) + land[0, 2].astype(F32) + land[1, 1].astype(F32)
    low = pair[ys[0], 32:64].astype(F32) + land[0, 1].astype(F32) + land[1, 2].astype(F32)
    done(jnp.concatenate([top, low], axis=0))


SQ = math.sqrt(2.0 / math.pi)
FAR_FIRST = (4, 3, 5, 2, 6, 1, 7, 0)
FB = WIDTH // BLK


def rows64(ref, h):
    return ref.at[pl.ds(h * 64, 64), :]


def step_kernel(scale, x_ref, up_ref, gain_ref, win_ref, wout_ref, bi_ref, seg_ref, teacher_ref, readout_ref,
                lo_ref, ig_ref, gin_ref, gout_ref,
                x_v, gain_v, table_v, nrm_all, up_all, win_all, wout_all, bi_all, bi,
                nrm_blocks, act_rows, act_t, slope, wide_out, wide_in, part,
                rs1, pair1, stage1, land1, ids, scores, coeffs,
                cot, pre, back, din, dout, rs, pair, stage, land,
                za_stage, za_land, za_sum, xb_land, xb_sum, zb_stage, zb_land,
                slab, dealt_in, dealt, send_sem, recv_sem, local_sem):
    p = Place()
    mail = Mail(send_sem, recv_sem)
    flows = Flows()
    local = []

    def keep(src, dst):
        copy = pltpu.make_async_copy(src, dst, local_sem.at[len(local)])
        copy.start()
        local.append(copy)
        return copy

    yplus, yminus = p.along("y", 1), p.along("y", -1)
    zplus, zminus = p.along("z", 1), p.along("z", -1)
    near = [p.flat(1), p.flat(-1)]
    eye = lax.broadcasted_iota(jnp.int32, (ROWS, BLK), 0) == lax.broadcasted_iota(jnp.int32, (ROWS, BLK), 1)
    loads = [keep(x_ref, x_v), keep(gain_ref, gain_v), keep(bi_ref, table_v), keep(up_ref, up_all.at[p.q])]

    def first():
        for copy in loads[:3]:
            copy.wait()
        wide = x_v[...].astype(F32)
        inv_rms = lax.rsqrt(jnp.mean(wide * wide, axis=1, keepdims=True) + EPS)
        nrm_all[p.q] = (wide * inv_rms * gain_v[...]).astype(BF16)
        bi_all[p.z] = jnp.zeros((8, BLK), jnp.int32)
        bi_all[p.z, 0:KB, 0:Z] = table_v[...]
        ids[0] = jnp.full((8, BLK), -1.0, F32)
        ids[0, 0:1, 0:ROWS] = seg_ref[...].astype(F32)
        loads[3].wait()

    greet([p.plane(dx, o) for dx in range(X) for o in range(Q) if dx or o] + [zplus, zminus] + near, first)
    id_copies = [mail.send(ids.at[0], ids.at[1 + i], near[i]) for i in (0, 1)]

    def columns(ref, q):
        return ref.at[:, pl.ds(pl.multiple_of(q * BLK, BLK), BLK)]

    def my_rows(ref):
        return ref.at[pl.ds(pl.multiple_of(p.q * 16, 16), 16), :]

    in_slab, out_slab = win_all.at[p.z, p.x], wout_all.at[p.x, p.z]
    in_deals, out_deals = {}, []
    for o in range(Q):
        q = lax.rem(p.q + o, Q)
        for dx in range(X):
            if dx or o:
                in_deals[dx, o] = mail.send(columns(win_ref, q), my_rows(in_slab), p.plane(dx, o))
        if o:
            out_deals.append(mail.send(columns(wout_ref, q), my_rows(out_slab), p.member(o)))
    slab_copies = [keep(columns(win_ref, p.q), my_rows(in_slab)), keep(columns(wout_ref, p.q), my_rows(out_slab))]

    def tokens(out, first):
        def half(y, h):
            return out.at[y * C + p.c, pl.ds(h * 32, 32), :]

        relays = []

        def pass_on(ref, to):
            relays.append(mail.send(ref, ref, to))
            return relays[-1]

        a0 = mail.send(half(p.y, 0), half(p.y, 0), yplus)
        b1 = mail.send(half(p.y, 1), half(p.y, 1), yminus)
        a1 = mail.send(half(p.y, 1), half(p.y, 1), yplus)
        b0 = mail.send(half(p.y, 0), half(p.y, 0), yminus)
        pass_on(out.at[p.q], p.sibling())
        left, right, far = lax.rem(p.y + 3, Y), lax.rem(p.y + 1, Y), lax.rem(p.y + 2, Y)
        yield first
        a0.wait_recv()
        fa = mail.send(half(left, 0), half(left, 0), yplus)
        pass_on(half(left, 0), p.sibling())
        b1.wait_recv()
        fb = mail.send(half(right, 1), half(right, 1), yminus)
        pass_on(half(right, 1), p.sibling())
        yield 3.0
        a1.wait_recv()
        pass_on(half(left, 1), p.sibling())
        b0.wait_recv()
        pass_on(half(right, 0), p.sibling())
        yield 8.3
        fa.wait_recv()
        pass_on(half(far, 0), p.sibling())
        fb.wait_recv()
        pass_on(half(far, 1), p.sibling())
        yield 2.0
        for copy in relays:
            copy.wait_recv()

    def table():
        mine = bi_all.at[p.z]
        a = mail.send(mine, mine, zplus)
        b = mail.send(mine, mine, zminus)
        for step in range(1, Z // 2 + 1):
            yield 2.5
            a.wait_recv()
            left = bi_all.at[lax.rem(p.z - step + Z, Z)]
            if step < Z // 2:
                a = mail.send(left, left, zplus)
                b.wait_recv()
                right = bi_all.at[lax.rem(p.z + step, Z)]
                if step < Z // 2 - 1:
                    b = mail.send(right, right, zminus)
        known = pltpu.make_async_copy(bi_all, bi, local_sem.at[7])
        known.start()
        known.wait()

    def w_in_z(k):
        return gather_ring(
            mail, Z, p.z, zplus, zminus,
            lambda z: win_all.at[z, k],
            lambda z, h: win_all.at[z, k, pl.ds(h * 64, 64), :],
            [3.0] * 4)

    def w_out_x(z):
        ref = wout_all.at[p.x, z]
        copies = [mail.send(ref, ref, p.along("x", dx)) for dx in (1, 2, 3)]
        yield 6.0
        for copy in copies:
            copy.wait_recv()

    def w_in():
        yield 2.5
        slab_copies[0].wait()
        for dx in range(X):
            for o in range(Q):
                if dx or o:
                    in_deals[dx, o].wait_recv()
            flows.add(w_in_z(lax.rem(p.x - dx + X, X)), ("w_in", dx))
            yield 0.3

    def w_out():
        yield 2.6
        slab_copies[1].wait()
        for copy in out_deals:
            copy.wait_recv()
        seen, begun = [], []

        def got(z, h):
            if h is not None:
                seen.append(h)
            if h is None or len(seen) == 2:
                begun.append(z)
                flows.add(w_out_x(z), ("w_out", len(begun)))

        flows.add(gather_ring(
            mail, Z, p.z, zplus, zminus,
            lambda z: wout_all.at[p.x, z],
            lambda z, h: wout_all.at[p.x, z, pl.ds(h * 64, 64), :],
            [2.5] * 4, got))
        flows.add(w_out_x(p.z), ("w_out", 0))


    def member_rows(y):
        return pl.ds(pl.multiple_of(y * (C * ROWS), C * ROWS), C * ROWS)

    def member(ref):
        return lambda q: ref.at[pl.ds(pl.multiple_of(q * ROWS, ROWS), ROWS), :]

    def widen(j, blocks, out):
        at = [bi[j, k, p.q] for k in range(KB)]
        cols = slice(j * BLK, (j + 1) * BLK)
        for d in range(FB):
            out[d * BLK:(d + 1) * BLK, cols] = sum(
                blocks[k] * (at[k] == d).astype(F32).astype(BF16) for k in range(KB))

    def product(lhs, wide, out):
        def make(ys):
            rows = jnp.concatenate([lhs[member_rows(y), :] for y in ys], axis=0)
            for n in range(4):
                cols = slice(n * 512, (n + 1) * 512)
                value = dot(rows, wide[cols, :], NT).astype(BF16)
                for i, y in enumerate(ys):
                    out[member_rows(y), cols] = value[i * C * ROWS:(i + 1) * C * ROWS]
        return make

    total = []

    def forward():
        for d in range(FB):
            nrm_blocks[d] = nrm_all[:, :, d * BLK:(d + 1) * BLK].reshape(Q * ROWS, BLK)
        for j in range(Z):
            at = [bi[j, k, p.q] for k in range(KB)]
            picked = jnp.concatenate([nrm_blocks[a] for a in at], axis=1)
            v = dot(picked, win_all[j].reshape(KB * BLK, BLK), NN)
            tanh = jnp.tanh(SQ * (v + 0.044715 * (v * v * v)))
            act = 0.5 * v * (1.0 + tanh)
            slope[j] = 0.5 * (1.0 + tanh) + 0.5 * v * (1.0 - tanh * tanh) * (SQ * (1.0 + 3.0 * 0.044715 * (v * v)))
            act_rows[:, j * BLK:(j + 1) * BLK] = act.astype(BF16)
            act_t[j] = act.T.astype(BF16)
            widen(j, [wout_all[k, j] for k in range(KB)], wide_out)
            yield 0.7
        yield from reduce_tokens(
            mail, p, product(act_rows, wide_out, part), member(part), rs1, pair1, stage1, land1,
            total.append, [1.0, 4.0, 4.0])

    def wide_weights():
        for j in range(Z):
            yield 0.4
            widen(j, [win_all[j, k] for k in range(KB)], wide_in)

    def score():
        lo = (x_v[...].astype(F32) + total[0]).astype(BF16)
        lo_ref[...] = lo
        token = jnp.sum(lo.astype(F32) * readout_ref[...], axis=1, keepdims=True)
        scores[0] = jnp.broadcast_to(jnp.sum(jnp.where(eye, token, 0.0), axis=0, keepdims=True), (8, BLK))
        copies = [mail.send(scores.at[0], scores.at[1 + i], near[i]) for i in (0, 1)]
        ids_col = jnp.sum(jnp.where(eye, ids[0, 0:1, :], 0.0), axis=1, keepdims=True)
        segs = teacher_ref.shape[1]
        hot = lax.broadcasted_iota(jnp.int32, (ROWS, segs), 1).astype(F32) == ids_col
        teacher = jnp.sum(jnp.where(hot, teacher_ref[...], 0.0), axis=1, keepdims=True)
        yield 2.5
        for copy in id_copies + copies:
            copy.wait_recv()
        sums = jnp.zeros((ROWS, 1), F32)
        counts = jnp.zeros((ROWS, 1), F32)
        for i in range(3):
            same = ids[i, 0:1, :] == ids_col
            sums += jnp.sum(jnp.where(same, scores[i, 0:1, :], 0.0), axis=1, keepdims=True)
            counts += jnp.sum(jnp.where(same, 1.0, 0.0), axis=1, keepdims=True)
        coeff = (2.0 * LOSS_WEIGHT) * (sums / counts - teacher)
        coeff_row = jnp.sum(jnp.where(eye, coeff, 0.0), axis=0, keepdims=True)
        coeffs[p.q] = jnp.broadcast_to(coeff_row, (8, BLK))
        out = [mail.send(coeffs.at[p.q], coeffs.at[p.q], p.member(o)) for o in range(1, Q)]
        yield 2.5
        for copy in out:
            copy.wait_recv()

    def cotangent(b):
        coeff = jnp.sum(jnp.where(eye, coeffs[b][0:1, :], 0.0), axis=1, keepdims=True)
        return (up_all[b].astype(F32) + coeff * readout_ref[...]).astype(BF16)

    def block(dz):
        j = lax.rem(p.z + dz, Z)
        at = [bi[j, k, p.q] for k in range(KB)]
        picked = jnp.concatenate([cot[a] for a in at], axis=1)
        chosen = jnp.concatenate([nrm_blocks[a] for a in at], axis=1)
        w_out = jnp.concatenate([wout_all[k, j] for k in range(KB)], axis=0)
        value = dot(picked, w_out, NN) * slope[j]
        pre[:, pl.ds(pl.multiple_of(j * BLK, BLK), BLK)] = value.astype(BF16)
        d_in = (dot(value.T.astype(BF16), chosen, NN) * scale).astype(BF16)
        d_out = (dot(act_t[j], picked, NN) * scale).astype(BF16)
        for k in range(KB):
            cols = slice(k * BLK, (k + 1) * BLK)
            din[dz, k] = d_in[:, cols]
            dout[dz, k] = d_out[:, cols]

    ready = set()
    grads, deals, x_sends = [], [], {}

    def out_x(dz):
        for dx in (1, 2, 3):
            x = lax.rem(p.x + dx, X)
            x_sends[dz, dx] = mail.send(dout.at[dz, x], xb_land.at[dx - 1, dz], p.along("x", dx))

    def in_z(dx):
        k = lax.rem(p.x + dx, X)

        def own(dz):
            assert dz in ready
            return din.at[dz, k]

        def done(value):
            za_sum[dx] = value.T.astype(BF16)
            for o in range(Q):
                rows = pl.ds(pl.multiple_of(lax.rem(p.q + o, Q) * 16, 16), 16)
                if dx == 0 and o == 0:
                    dealt_in[p.x, p.q] = za_sum[dx, rows, :]
                else:
                    deals.append(mail.send(za_sum.at[dx, rows, :], dealt_in.at[p.x, p.q], p.plane(dx, o)))

        return reduce_ring(
            mail, Z, zplus, zminus, own, rows64,
            lambda way, step: za_stage.at[dx, way, step - 2], lambda way, step: za_land.at[dx, way, step - 1],
            [3.2] * 4, done)

    summed = set()

    def out_own(dz):
        if dz not in summed:
            assert dz in ready
            summed.add(dz)
            for dx in (1, 2, 3):
                x_sends[dz, dx].wait_recv()
            value = dout[dz, p.x].astype(F32) + sum(xb_land[i, dz].astype(F32) for i in range(3))
            xb_sum[dz] = value.astype(BF16)
        return xb_sum.at[dz]

    def deal(value):
        slab[...] = value.T.astype(BF16)
        dealt[p.q] = slab[pl.ds(pl.multiple_of(p.q * 16, 16), 16), :]
        for o in range(1, Q):
            rows = slab.at[pl.ds(pl.multiple_of(lax.rem(p.q + o, Q) * 16, 16), 16), :]
            deals.append(mail.send(rows, dealt.at[p.q], p.member(o)))

    def out_z():
        yield 3.5
        yield from reduce_ring(
            mail, Z, zplus, zminus, out_own, rows64,
            lambda way, step: zb_stage.at[way, step - 2], lambda way, step: zb_land.at[way, step - 1],
            [3.0, 3.0, 3.0, 3.0], deal)

    def compute():
        for b in range(Q):
            value = cotangent(b)
            for d in range(FB):
                cot[d, b * ROWS:(b + 1) * ROWS, :] = value[:, d * BLK:(d + 1) * BLK]
        for dz in FAR_FIRST:
            block(dz)
            ready.add(dz)
            out_x(dz)
            if dz == FAR_FIRST[0]:
                for dx in (1, 2, 3, 0):
                    flows.add(in_z(dx))
                flows.add(out_z())
            yield 1.0
        yield from reduce_tokens(
            mail, p, product(pre, wide_in, back), member(back), rs, pair, stage, land,
            grads.append, [1.0, 5.0, 6.0])

    flows.add(w_in())
    flows.add(w_out())
    flows.add(tokens(nrm_all, 4.5), "normed")
    flows.add(tokens(up_all, 10.0), "upstream")
    flows.add(table(), "table")
    gathered = ["normed", "table"] + [("w_in", i) for i in range(X)] + [("w_out", i) for i in range(Z)]
    flows.after(gathered, lambda: (flows.add(forward(), "forward"), flows.add(wide_weights(), "wide")))
    flows.after(["forward"], lambda: flows.add(score(), "score"))
    flows.after(["score", "upstream", "wide"], lambda: flows.add(compute()))
    flows.run()

    wide = x_v[...].astype(F32)
    inv = lax.rsqrt(jnp.mean(wide * wide, axis=1, keepdims=True) + EPS)
    scaled = grads[0] * gain_v[...]
    inner = jnp.mean(scaled * wide, axis=1, keepdims=True)
    ig_ref[...] = (cotangent(p.q).astype(F32) + (inv * scaled - wide * (inv * inv * inv) * inner)).astype(BF16)
    for copy in deals:
        copy.wait_recv()
    for q in range(Q):
        cols = slice(q * BLK, (q + 1) * BLK)
        gin_ref[:, cols] = sum(dealt_in[x, q].astype(F32) for x in range(X))
        gout_ref[:, cols] = dealt[q].astype(F32)
    mail.close()


def step(scale, *arrays):
    n = Q * ROWS
    tile = (BLK, BLK)
    far = pl.BlockSpec(memory_space=pltpu.HBM)

    def token_buffers():
        return [
            pltpu.VMEM((Y, ROWS, WIDTH), BF16),
            pltpu.VMEM((Y, ROWS, WIDTH), BF16),
            pltpu.VMEM((2, ROWS // 2, WIDTH), BF16),
            pltpu.VMEM((2, 3, ROWS // 2, WIDTH), BF16),
        ]

    return pl.pallas_call(
        functools.partial(step_kernel, scale),
        name="step",
        out_shape=(
            jax.ShapeDtypeStruct((ROWS, WIDTH), BF16),
            jax.ShapeDtypeStruct((ROWS, WIDTH), BF16),
            jax.ShapeDtypeStruct((16, Q * BLK), F32),
            jax.ShapeDtypeStruct((16, Q * BLK), F32),
        ),
        in_specs=[far] * 6 + [VM] * 3,
        out_specs=(VM,) * 4,
        scratch_shapes=[
            pltpu.VMEM((ROWS, WIDTH), BF16),
            pltpu.VMEM((1, WIDTH), F32),
            pltpu.VMEM((KB, Z), jnp.int32),
            pltpu.VMEM((Q, ROWS, WIDTH), BF16),
            pltpu.VMEM((Q, ROWS, WIDTH), BF16),
            pltpu.VMEM((Z, KB) + tile, BF16),
            pltpu.VMEM((KB, Z) + tile, BF16),
            pltpu.VMEM((Z, 8, BLK), jnp.int32),
            pltpu.SMEM((Z, 8, BLK), jnp.int32),
            pltpu.VMEM((FB, n, BLK), BF16),
            pltpu.VMEM((n, Z * BLK), BF16),
            pltpu.VMEM((Z, BLK, n), BF16),
            pltpu.VMEM((Z, n, BLK), F32),
            pltpu.VMEM((WIDTH, Z * BLK), BF16),
            pltpu.VMEM((WIDTH, Z * BLK), BF16),
            pltpu.VMEM((n, WIDTH), BF16),
            *token_buffers(),
            pltpu.VMEM((3, 8, BLK), F32),
            pltpu.VMEM((3, 8, BLK), F32),
            pltpu.VMEM((Q, 8, BLK), F32),
            pltpu.VMEM((FB, n, BLK), BF16),
            pltpu.VMEM((n, Z * BLK), BF16),
            pltpu.VMEM((n, WIDTH), BF16),
            pltpu.VMEM((Z, KB) + tile, BF16),
            pltpu.VMEM((Z, KB) + tile, BF16),
            *token_buffers(),
            pltpu.VMEM((KB, 2, 3) + tile, BF16),
            pltpu.VMEM((KB, 2, 4) + tile, BF16),
            pltpu.VMEM((KB,) + tile, BF16),
            pltpu.VMEM((3, Z) + tile, BF16),
            pltpu.VMEM((Z,) + tile, BF16),
            pltpu.VMEM((2, 3) + tile, BF16),
            pltpu.VMEM((2, 4) + tile, BF16),
            pltpu.VMEM(tile, BF16),
            pltpu.VMEM((X, Q, 16, BLK), BF16),
            pltpu.VMEM((Q, 16, BLK), BF16),
            pltpu.SemaphoreType.DMA((288,)),
            pltpu.SemaphoreType.DMA((288,)),
            pltpu.SemaphoreType.DMA((8,)),
        ],
        compiler_params=pltpu.CompilerParams(collective_id=0, has_side_effects=True, vmem_limit_bytes=60 << 20),
    )(*arrays)


def on_device(
    inputs, norm_gain, w_in, w_out, block_index, segment_ids, teacher_scores, upstream, readout
):
    scale = 1.0 / math.sqrt(ROWS * X * Q * Z)
    remote = [pltpu.with_memory_space_constraint(a, pltpu.HBM)
              for a in (inputs, upstream, norm_gain[None, :], w_in, w_out, block_index.T)]
    return step(scale, *remote, segment_ids[None, :], teacher_scores[None, :], readout[None, :])


def solution(mesh):
    return jax.shard_map(
        on_device,
        mesh=mesh,
        in_specs=(
            P(("tok", "feat"), None),
            P(),
            P("tok", "feat"),
            P("tok", "feat"),
            P("feat", None),
            P(("tok", "feat")),
            P(),
            P(("tok", "feat"), None),
            P(),
        ),
        out_specs=(
            P(("tok", "feat"), None),
            P(("tok", "feat"), None),
            P("tok", "feat"),
            P("tok", "feat"),
        ),
        check_vma=False,
    )
```

time: 583 us -> 105 us (0.18)
  waiting for transfers between devices: 393 us -> 0 us
  Pallas kernels: 0 us -> 100 us
  blocking collectives: 79 us -> 0 us
  matrix products: 38.3 us -> 0 us
  local copies, waits for them, and re-layouts: 41 us -> 4.07 us
  between operations: 14.4 us -> 0.65 us
  other arithmetic: 11 us -> 0 us
    reduce_scatter x4 -> x0, waiting for transfers between devices: 224 us -> none  [the longest x1 87.3 us: on_device(): lax.psum_scatter(arrange(out_terms).astype(jnp.bfloat16), 'tok', scatter_...]
    all_gather x4 -> x0, waiting for transfers between devices: 168 us -> none  [the longest x1 50.6 us: on_device(): lax.all_gather(w_in, 'tok', axis=0, tiled=True)]
    pallas_call x0 -> x1, Pallas kernels: none -> 100 us  [step(): pl.pallas_call(functools.partial(step_kernel, scale), name='step', out_sh...]
    psum x1 -> x0, blocking collectives: 79 us -> none  [on_device(): lax.psum((score_sums, token_counts), ('tok', 'feat'))]
    dot_general x12 -> x0, matrix products: 38.3 us -> none  [the longest x2 11.2 us: spread(): jnp.einsum('rjkc,jkd->rdc', grouped, sel_wide, precision=lax.Precision.HI...]
    reshape x2 -> x0, local copies, waits for them, and re-layouts: 20.9 us -> none  [spread(): grouped = terms.reshape(group_rows, blocks_here, per_hidden, BLK)]
    convert_element_type x6 -> x0, other arithmetic: 8.4 us -> none  [the longest x2 2.78 us: on_device(): grad_out, grad_in = (lax.psum_scatter(arrange(out_terms).astype(jnp.bfloa...]
    unnamed x38 -> x10, local copies, waits for them, and re-layouts: 10.9 us -> 4.07 us
  transfers between devices with their start and end apart: 8 -> 0, of which waited for: 8 -> 0; matrix products, arithmetic and copies ran while one was open for 7% -> 0% of each run, Pallas kernels for 0% -> 0%
where the time goes in v3:
time: 105 us
  Pallas kernels  100 us (95%)
  local copies, waits for them, and re-layouts  4.07 us (4%)
    pallas_call x1, Pallas kernels, step(): pl.pallas_call(functools.partial(step_kernel, scale), name='step', out_sh...  100 us
    unnamed x10, local copies, waits for them, and re-layouts  4.07 us

profile of v3, /device:TPU:1, one launch (start us, length us, event | category | flops | bytes accessed | tf_op | source)
XLA Modules:
  0.0 105.0 jit_solution(13680541707113870253)
XLA Ops:
  0.6 100.2 %step.1 = (bf16[64,2048]{1,0:T(8,128)(2,1)}, bf16[64,2048]{1,0:T(8,128)(2,1)}, f32[16,1024]{1,0:T(8,128)}, f32[16,1024]{1,0:T(8,128)}) custom-call(bf16[64,2048]{1,0:T(8,128)(2,1)} %x_ref.1, bf16[64,2048]{1,0:T(8,128)(2,1)} %up_ref.1, f32[1,2048]{1,0:T(1,128)} %bitcast.5, bf16[16,1024]{1,0:T(8,128)(2,1)} %win_ref.1, bf16[16,1024]{1,0:T(8,128)(2,1)} %wout_ref.1, ...), custom_call_target="tpu_custom_call" | custom-call | tf_op jit(solution)/shard_map/step/pallas_call | solution.py:599
  100.9 0.0 copy-start
  100.9 1.7 %copy.17 = bf16[64,2048]{1,0:T(8,128)(2,1)} copy(bf16[64,2048]{1,0:T(8,128)(2,1)} %get-tuple-element.8) | data formatting | bytes 524288
  102.6 0.0 copy-done
  102.6 0.0 copy-start.2
  102.6 0.7 copy.18
  103.3 0.2 copy-done.2
  103.5 0.0 copy-start.1
  103.5 0.6 copy.19
  104.1 0.2 copy-done.1
  104.3 0.6 copy.20
Async XLA Ops:
  100.9 1.7 %copy-start = (bf16[64,2048]{1,0:T(8,128)(2,1)S(1)}, bf16[64,2048]{1,0:T(8,128)(2,1)}, u32[]{:S(2)}) copy-start(bf16[64,2048]{1,0:T(8,128)(2,1)} %get-tuple-element.9) | copy-start | bytes 786436
  102.6 0.9 copy-start.2
  103.5 0.9 copy-start.1

commit v4 on v3

--- a/solution.py
+++ b/solution.py
@@ -17,6 +17,7 @@
 ROWS = 64
 WIDTH = 2048
 KB = 4
+SEGMENTS = 1024
 MESH = pl.DeviceIdType.MESH
 F32, BF16 = jnp.float32, jnp.bfloat16
 NT = (((1,), (1,)), ((), ()))
@@ -140,18 +141,18 @@
             ref = half(left, 0) if step == n // 2 - 1 else piece(left)
             a = mail.send(ref, ref, plus)
             if arrived:
-                arrived(left, None)
+                arrived(left, None, n - step)
         elif arrived:
-            arrived(left, 0)
+            arrived(left, 0, n - step)
         b.wait_recv()
         right = lax.rem(me + step, n)
         if not last:
             ref = half(right, 1) if step == n // 2 - 1 else piece(right)
             b = mail.send(ref, ref, minus)
             if arrived:
-                arrived(right, None)
+                arrived(right, None, step)
         elif arrived:
-            arrived(right, 1)
+            arrived(right, 1, step)
 
 
 def reduce_ring(mail, n, plus, minus, own, half, stage, land, delays, done):
@@ -189,8 +190,8 @@
     other = 1 - p.c
     sends = {}
     ys = [lax.rem(p.y + o, Y) for o in range(Y)]
-    for two in ((2, 1), (3, 0)):
-        make([ys[o] for o in two])
+    for two in ((2, 1, 3, 0),):
+        yield from make([ys[o] for o in two])
         for o in two:
             sends[o] = mail.send(part(ys[o] * C + other), rs.at[ys[o]], p.sibling())
         yield 0.2
@@ -233,9 +234,9 @@
     return ref.at[pl.ds(h * 64, 64), :]
 
 
-def step_kernel(scale, x_ref, up_ref, gain_ref, win_ref, wout_ref, bi_ref, seg_ref, teacher_ref, readout_ref,
+def step_kernel(scale, x_ref, up_ref, gain_ref, win_ref, wout_ref, bi_ref, seg_hbm, teacher_hbm, readout_hbm,
                 lo_ref, ig_ref, gin_ref, gout_ref,
-                x_v, gain_v, table_v, nrm_all, up_all, win_all, wout_all, bi_all, bi,
+                x_v, gain_v, table_v, seg_ref, teacher_ref, readout_ref, nrm_all, up_all, win_all, wout_all, bi_all, bi,
                 nrm_blocks, act_rows, act_t, slope, wide_out, wide_in, part,
                 rs1, pair1, stage1, land1, ids, scores, coeffs,
                 cot, pre, back, din, dout, rs, pair, stage, land,
@@ -256,10 +257,11 @@
     zplus, zminus = p.along("z", 1), p.along("z", -1)
     near = [p.flat(1), p.flat(-1)]
     eye = lax.broadcasted_iota(jnp.int32, (ROWS, BLK), 0) == lax.broadcasted_iota(jnp.int32, (ROWS, BLK), 1)
-    loads = [keep(x_ref, x_v), keep(gain_ref, gain_v), keep(bi_ref, table_v), keep(up_ref, up_all.at[p.q])]
+    loads = [keep(x_ref, x_v), keep(gain_ref, gain_v), keep(bi_ref, table_v), keep(seg_hbm, seg_ref),
+             keep(teacher_hbm, teacher_ref), keep(readout_hbm, readout_ref), keep(up_ref, up_all.at[p.q])]
 
     def first():
-        for copy in loads[:3]:
+        for copy in loads[:4]:
             copy.wait()
         wide = x_v[...].astype(F32)
         inv_rms = lax.rsqrt(jnp.mean(wide * wide, axis=1, keepdims=True) + EPS)
@@ -268,7 +270,8 @@
         bi_all[p.z, 0:KB, 0:Z] = table_v[...]
         ids[0] = jnp.full((8, BLK), -1.0, F32)
         ids[0, 0:1, 0:ROWS] = seg_ref[...].astype(F32)
-        loads[3].wait()
+        for copy in loads[4:]:
+            copy.wait()
 
     greet([p.plane(dx, o) for dx in range(X) for o in range(Q) if dx or o] + [zplus, zminus] + near, first)
     id_copies = [mail.send(ids.at[0], ids.at[1 + i], near[i]) for i in (0, 1)]
@@ -341,16 +344,23 @@
                 right = bi_all.at[lax.rem(p.z + step, Z)]
                 if step < Z // 2 - 1:
                     b = mail.send(right, right, zminus)
-        known = pltpu.make_async_copy(bi_all, bi, local_sem.at[7])
+        known = pltpu.make_async_copy(bi_all, bi, local_sem.at[11])
         known.start()
         known.wait()
+
+    arrivals = {}
+
+    def got_in(z, h, d):
+        arrivals[d] = arrivals.get(d, 0) + 1
+        if arrivals[d] == (KB if h is None else 2 * KB):
+            flows.end(("w_in", d))
 
     def w_in_z(k):
         return gather_ring(
             mail, Z, p.z, zplus, zminus,
             lambda z: win_all.at[z, k],
             lambda z, h: win_all.at[z, k, pl.ds(h * 64, 64), :],
-            [3.0] * 4)
+            [3.0] * 4, got_in)
 
     def w_out_x(z):
         ref = wout_all.at[p.x, z]
@@ -366,22 +376,22 @@
             for o in range(Q):
                 if dx or o:
                     in_deals[dx, o].wait_recv()
-            flows.add(w_in_z(lax.rem(p.x - dx + X, X)), ("w_in", dx))
+            flows.add(w_in_z(lax.rem(p.x - dx + X, X)))
             yield 0.3
+        flows.end(("w_in", 0))
 
     def w_out():
         yield 2.6
         slab_copies[1].wait()
         for copy in out_deals:
             copy.wait_recv()
-        seen, begun = [], []
-
-        def got(z, h):
+        seen = []
+
+        def got(z, h, d):
             if h is not None:
                 seen.append(h)
             if h is None or len(seen) == 2:
-                begun.append(z)
-                flows.add(w_out_x(z), ("w_out", len(begun)))
+                flows.add(w_out_x(z), ("w_out", d))
 
         flows.add(gather_ring(
             mail, Z, p.z, zplus, zminus,
@@ -398,7 +408,7 @@
         return lambda q: ref.at[pl.ds(pl.multiple_of(q * ROWS, ROWS), ROWS), :]
 
     def widen(j, blocks, out):
-        at = [bi[j, k, p.q] for k in range(KB)]
+        at = [bi[lax.rem(p.z + j, Z), k, p.q] for k in range(KB)]
         cols = slice(j * BLK, (j + 1) * BLK)
         for d in range(FB):
             out[d * BLK:(d + 1) * BLK, cols] = sum(
@@ -412,32 +422,40 @@
                 value = dot(rows, wide[cols, :], NT).astype(BF16)
                 for i, y in enumerate(ys):
                     out[member_rows(y), cols] = value[i * C * ROWS:(i + 1) * C * ROWS]
+                yield 0.5
         return make
 
     total = []
 
-    def forward():
+    def blocks():
         for d in range(FB):
             nrm_blocks[d] = nrm_all[:, :, d * BLK:(d + 1) * BLK].reshape(Q * ROWS, BLK)
-        for j in range(Z):
-            at = [bi[j, k, p.q] for k in range(KB)]
-            picked = jnp.concatenate([nrm_blocks[a] for a in at], axis=1)
-            v = dot(picked, win_all[j].reshape(KB * BLK, BLK), NN)
-            tanh = jnp.tanh(SQ * (v + 0.044715 * (v * v * v)))
-            act = 0.5 * v * (1.0 + tanh)
-            slope[j] = 0.5 * (1.0 + tanh) + 0.5 * v * (1.0 - tanh * tanh) * (SQ * (1.0 + 3.0 * 0.044715 * (v * v)))
-            act_rows[:, j * BLK:(j + 1) * BLK] = act.astype(BF16)
-            act_t[j] = act.T.astype(BF16)
-            widen(j, [wout_all[k, j] for k in range(KB)], wide_out)
-            yield 0.7
+        yield 0.3
+
+    def forward_block(d):
+        j = lax.rem(p.z + d, Z)
+        at = [bi[j, k, p.q] for k in range(KB)]
+        picked = jnp.concatenate([nrm_blocks[a] for a in at], axis=1)
+        v = dot(picked, win_all[j].reshape(KB * BLK, BLK), NN)
+        tanh = jnp.tanh(SQ * (v + 0.044715 * (v * v * v)))
+        act = 0.5 * v * (1.0 + tanh)
+        slope[d] = 0.5 * (1.0 + tanh) + 0.5 * v * (1.0 - tanh * tanh) * (SQ * (1.0 + 3.0 * 0.044715 * (v * v)))
+        act_rows[:, d * BLK:(d + 1) * BLK] = act.astype(BF16)
+        act_t[d] = act.T.astype(BF16)
+        yield 0.5
+        widen(d, [wout_all[k, j] for k in range(KB)], wide_out)
+        yield 0.3
+
+    def forward():
         yield from reduce_tokens(
             mail, p, product(act_rows, wide_out, part), member(part), rs1, pair1, stage1, land1,
             total.append, [1.0, 4.0, 4.0])
 
     def wide_weights():
-        for j in range(Z):
+        yield 4.5
+        for d in range(Z):
+            widen(d, [win_all[lax.rem(p.z + d, Z), k] for k in range(KB)], wide_in)
             yield 0.4
-            widen(j, [win_all[j, k] for k in range(KB)], wide_in)
 
     def score():
         lo = (x_v[...].astype(F32) + total[0]).astype(BF16)
@@ -476,10 +494,12 @@
         picked = jnp.concatenate([cot[a] for a in at], axis=1)
         chosen = jnp.concatenate([nrm_blocks[a] for a in at], axis=1)
         w_out = jnp.concatenate([wout_all[k, j] for k in range(KB)], axis=0)
-        value = dot(picked, w_out, NN) * slope[j]
-        pre[:, pl.ds(pl.multiple_of(j * BLK, BLK), BLK)] = value.astype(BF16)
+        value = dot(picked, w_out, NN) * slope[dz]
+        pre[:, dz * BLK:(dz + 1) * BLK] = value.astype(BF16)
+        yield 0.4
         d_in = (dot(value.T.astype(BF16), chosen, NN) * scale).astype(BF16)
-        d_out = (dot(act_t[j], picked, NN) * scale).astype(BF16)
+        yield 0.3
+        d_out = (dot(act_t[dz], picked, NN) * scale).astype(BF16)
         for k in range(KB):
             cols = slice(k * BLK, (k + 1) * BLK)
             din[dz, k] = d_in[:, cols]
@@ -512,7 +532,7 @@
         return reduce_ring(
             mail, Z, zplus, zminus, own, rows64,
             lambda way, step: za_stage.at[dx, way, step - 2], lambda way, step: za_land.at[dx, way, step - 1],
-            [3.2] * 4, done)
+            [4.5] * 4, done)
 
     summed = set()
 
@@ -538,7 +558,7 @@
         yield from reduce_ring(
             mail, Z, zplus, zminus, out_own, rows64,
             lambda way, step: zb_stage.at[way, step - 2], lambda way, step: zb_land.at[way, step - 1],
-            [3.0, 3.0, 3.0, 3.0], deal)
+            [4.0] * 4, deal)
 
     def compute():
         for b in range(Q):
@@ -546,14 +566,14 @@
             for d in range(FB):
                 cot[d, b * ROWS:(b + 1) * ROWS, :] = value[:, d * BLK:(d + 1) * BLK]
         for dz in FAR_FIRST:
-            block(dz)
+            yield from block(dz)
             ready.add(dz)
             out_x(dz)
             if dz == FAR_FIRST[0]:
                 for dx in (1, 2, 3, 0):
                     flows.add(in_z(dx))
                 flows.add(out_z())
-            yield 1.0
+            yield 0.3
         yield from reduce_tokens(
             mail, p, product(pre, wide_in, back), member(back), rs, pair, stage, land,
             grads.append, [1.0, 5.0, 6.0])
@@ -563,8 +583,12 @@
     flows.add(tokens(nrm_all, 4.5), "normed")
     flows.add(tokens(up_all, 10.0), "upstream")
     flows.add(table(), "table")
-    gathered = ["normed", "table"] + [("w_in", i) for i in range(X)] + [("w_out", i) for i in range(Z)]
-    flows.after(gathered, lambda: (flows.add(forward(), "forward"), flows.add(wide_weights(), "wide")))
+    flows.after(["normed"], lambda: flows.add(blocks(), "blocks"))
+    for d in range(Z):
+        flows.after(["blocks", "table", ("w_in", d), ("w_out", d)],
+                    lambda d=d: flows.add(forward_block(d), ("act", d)))
+    flows.after([("act", d) for d in range(Z)],
+                lambda: (flows.add(forward(), "forward"), flows.add(wide_weights(), "wide")))
     flows.after(["forward"], lambda: flows.add(score(), "score"))
     flows.after(["score", "upstream", "wide"], lambda: flows.add(compute()))
     flows.run()
@@ -605,12 +629,15 @@
             jax.ShapeDtypeStruct((16, Q * BLK), F32),
             jax.ShapeDtypeStruct((16, Q * BLK), F32),
         ),
-        in_specs=[far] * 6 + [VM] * 3,
+        in_specs=[far] * 9,
         out_specs=(VM,) * 4,
         scratch_shapes=[
             pltpu.VMEM((ROWS, WIDTH), BF16),
             pltpu.VMEM((1, WIDTH), F32),
             pltpu.VMEM((KB, Z), jnp.int32),
+            pltpu.VMEM((1, ROWS), jnp.int32),
+            pltpu.VMEM((1, SEGMENTS), F32),
+            pltpu.VMEM((1, WIDTH), F32),
             pltpu.VMEM((Q, ROWS, WIDTH), BF16),
             pltpu.VMEM((Q, ROWS, WIDTH), BF16),
             pltpu.VMEM((Z, KB) + tile, BF16),
@@ -646,9 +673,31 @@
             pltpu.VMEM((Q, 16, BLK), BF16),
             pltpu.SemaphoreType.DMA((288,)),
             pltpu.SemaphoreType.DMA((288,)),
-            pltpu.SemaphoreType.DMA((8,)),
+            pltpu.SemaphoreType.DMA((12,)),
         ],
-        compiler_params=pltpu.CompilerParams(collective_id=0, has_side_effects=True, vmem_limit_bytes=60 << 20),
+        compiler_params=pltpu.CompilerParams(collective_id=0, has_side_effects=True, vmem_limit_bytes=46 << 20),
+    )(*arrays)
+
+
+def emit_kernel(*refs):
+    sems = refs[-1]
+    n = (len(refs) - 1) // 2
+    copies = [pltpu.make_async_copy(refs[i], refs[n + i], sems.at[i]) for i in range(n)]
+    for copy in copies:
+        copy.start()
+    for copy in copies:
+        copy.wait()
+
+
+def emit(*arrays):
+    return pl.pallas_call(
+        emit_kernel,
+        name="emit",
+        out_shape=tuple(jax.ShapeDtypeStruct(a.shape, a.dtype) for a in arrays),
+        in_specs=[ANY] * len(arrays),
+        out_specs=(pl.BlockSpec(memory_space=pltpu.HBM),) * len(arrays),
+        scratch_shapes=[pltpu.SemaphoreType.DMA((len(arrays),))],
+        compiler_params=pltpu.CompilerParams(vmem_limit_bytes=1 << 20),
     )(*arrays)
 
 
@@ -657,8 +706,9 @@
 ):
     scale = 1.0 / math.sqrt(ROWS * X * Q * Z)
     remote = [pltpu.with_memory_space_constraint(a, pltpu.HBM)
-              for a in (inputs, upstream, norm_gain[None, :], w_in, w_out, block_index.T)]
-    return step(scale, *remote, segment_ids[None, :], teacher_scores[None, :], readout[None, :])
+              for a in (inputs, upstream, norm_gain[None, :], w_in, w_out, block_index.T,
+                        segment_ids[None, :], teacher_scores[None, :], readout[None, :])]
+    return emit(*step(scale, *remote))
 
 
 def solution(mesh):

time: 105 us -> 93.2 us (0.89)
  Pallas kernels: 100 us -> 92.3 us
  local copies, waits for them, and re-layouts: 4.07 us -> 0 us
    pallas_call x1, Pallas kernels: 100 us -> 91.4 us  [step(): pl.pallas_call(functools.partial(step_kernel, scale), name='step', out_sh...]
    unnamed x10 -> x0, local copies, waits for them, and re-layouts: 4.07 us -> none
where the time goes in v4:
time: 93.2 us; the launch traced here: 93.1 us
  Pallas kernels  92.3 us (99%)
    pallas_call x1, Pallas kernels, step(): pl.pallas_call(functools.partial(step_kernel, scale), name='step', out_sh...  91.4 us

profile of v4, /device:TPU:1, one launch (start us, length us, event | category | flops | bytes accessed | tf_op | source)
XLA Modules:
  0.0 93.1 jit_solution(12020782253220918748)
XLA Ops:
  0.6 91.4 %step.1 = (bf16[64,2048]{1,0:T(8,128)(2,1)S(1)}, bf16[64,2048]{1,0:T(8,128)(2,1)S(1)}, f32[16,1024]{1,0:T(8,128)S(1)}, f32[16,1024]{1,0:T(8,128)S(1)}) custom-call(bf16[64,2048]{1,0:T(8,128)(2,1)} %x_ref.1, bf16[64,2048]{1,0:T(8,128)(2,1)} %up_ref.1, f32[1,2048]{1,0:T(1,128)} %bitcast.5, bf16[16,1024]{1,0:T(8,128)(2,1)} %win_ref.1, ...), custom_call_target="tpu_custom_call" | custom-call | tf_op jit(solution)/shard_map/step/pallas_call | solution.py:623
  92.1 0.9 emit.1

commit v5 on v4

--- a/solution.py
+++ b/solution.py
@@ -576,12 +576,12 @@
             yield 0.3
         yield from reduce_tokens(
             mail, p, product(pre, wide_in, back), member(back), rs, pair, stage, land,
-            grads.append, [1.0, 5.0, 6.0])
+            grads.append, [1.0, 6.5, 8.0])
 
     flows.add(w_in())
     flows.add(w_out())
     flows.add(tokens(nrm_all, 4.5), "normed")
-    flows.add(tokens(up_all, 10.0), "upstream")
+    flows.add(tokens(up_all, 14.0), "upstream")
     flows.add(table(), "table")
     flows.after(["normed"], lambda: flows.add(blocks(), "blocks"))
     for d in range(Z):

time: 93.2 us -> 92.8 us (level)
  no operation moved by 1% of the time
where the time goes in v5:
time: 92.8 us; the launch traced here: 92.7 us
  Pallas kernels  91.9 us (99%)
    pallas_call x1, Pallas kernels, step(): pl.pallas_call(functools.partial(step_kernel, scale), name='step', out_sh...  91 us

profile of v5, /device:TPU:1, one launch (start us, length us, event | category | flops | bytes accessed | tf_op | source)
XLA Modules:
  0.0 92.7 jit_solution(9834916959118752082)
XLA Ops:
  0.6 91.0 %step.1 = (bf16[64,2048]{1,0:T(8,128)(2,1)S(1)}, bf16[64,2048]{1,0:T(8,128)(2,1)S(1)}, f32[16,1024]{1,0:T(8,128)S(1)}, f32[16,1024]{1,0:T(8,128)S(1)}) custom-call(bf16[64,2048]{1,0:T(8,128)(2,1)} %x_ref.1, bf16[64,2048]{1,0:T(8,128)(2,1)} %up_ref.1, f32[1,2048]{1,0:T(1,128)} %bitcast.5, bf16[16,1024]{1,0:T(8,128)(2,1)} %win_ref.1, ...), custom_call_target="tpu_custom_call" | custom-call | tf_op jit(solution)/shard_map/step/pallas_call | solution.py:623
  91.7 0.9 emit.1
